TPU v7x, 32 devices: a whole 2x2x4 slice. The times are simulated.
32 devices in a mesh: grp: 2 (over x), seqa: 8 (over z, y), seqb: 2 (over core).
Axes of the slice: x: 2, y: 2, z: 4, core: 2. Of those that a mesh axis runs over, the one named last changes fastest.
Arguments:
- inputs: bfloat16 [128, 256, 768], P(('grp', 'seqa', 'seqb')), parts along dimension 0, may hold values from -6 to 6
- out_grad: bfloat16 [128, 256, 768], P(('grp', 'seqa', 'seqb')), parts along dimension 0, may hold values from -24 to 24
- w_query: bfloat16 [768, 768], replicated, may hold values from -0.21875 to 0.21875
- w_key: bfloat16 [768, 768], replicated, may hold values from -0.21875 to 0.21875
- w_value: bfloat16 [768, 768], replicated, may hold values from -0.21875 to 0.21875
- w_output: bfloat16 [768, 768], replicated, may hold values from -0.21875 to 0.21875
- saved_probs: float32 [512, 12, 256], P('grp'), parts along dimension 0, may hold values from 0 to 1, as said below
Outputs:
- input_grad: float32 [128, 256, 768], P(('grp', 'seqa', 'seqb')), parts along dimension 0
There are 2 independent parts, one for each index of `grp`. A program takes and returns all parts, laid end to end along the dimension named above; an argument that names none is the same for every part. Nothing has to cross between parts.
Inputs may be any that keep to these rules, and one draw needn't show every extreme that they name: `saved_probs`: for every query residue and head, the 256 weights over key residues are positive and sum to one.
All inputs are finite; a program needn't handle non-finite values.
Results may differ from a plain program's by a relative error of at most 0.018.
Values may be sent and summed in bfloat16 or wider, within the bound.
No kernel may reach another device: no remote copies, remote signals or barrier semaphores. Data moves between devices by JAX's collectives and lax.ppermute only.
A program may use at most 64 MiB of HBM per device.

v0:
```python
import jax
import jax.numpy as jnp
from jax import lax
from jax.sharding import PartitionSpec as P


def transposed_product(left, weight):
    return lax.dot_general(
        left, weight, (((1,), (1,)), ((), ())), preferred_element_type=jnp.float32
    )


def local(inputs, out_grad, w_query, w_key, w_value, w_output, saved_probs):
    seq_dev, length, width = inputs.shape
    heads = saved_probs.shape[1]
    head_size = width // heads
    total_seqs = seq_dev * lax.axis_size("seqa") * lax.axis_size("seqb")
    scale = (head_size * total_seqs) ** (-0.5)

    def shaped(flat_rows):
        return flat_rows.astype(jnp.bfloat16).reshape(seq_dev, length, heads, head_size)

    flat_in = inputs.reshape(-1, width)
    values = shaped(jnp.dot(flat_in, w_value, preferred_element_type=jnp.float32))
    attn_grad = shaped(transposed_product(out_grad.reshape(-1, width), w_output))
    queries = shaped(jnp.dot(flat_in, w_query, preferred_element_type=jnp.float32))
    key_rows = shaped(jnp.dot(flat_in, w_key, preferred_element_type=jnp.float32))
    row_count = length // (lax.axis_size("seqa") * lax.axis_size("seqb"))
    share = lax.psum_scatter(
        jnp.einsum("sihe,sjhe->ihj", attn_grad, values, preferred_element_type=jnp.float32).astype(
            jnp.bfloat16
        ),
        ("seqa", "seqb"),
        scatter_dimension=0,
        tiled=True,
    ).astype(jnp.float32)
    probs = lax.dynamic_slice_in_dim(
        saved_probs, lax.axis_index(("seqa", "seqb")) * row_count, share.shape[0], 0
    )
    inner = jnp.sum(probs * share, axis=-1, keepdims=True)
    own_rows = (probs * (share - inner)).astype(jnp.bfloat16)
    logit_grad = lax.all_gather(own_rows, ("seqa", "seqb"), axis=0, tiled=True)
    probs_low = saved_probs.astype(jnp.bfloat16)
    query_grad = (
        scale
        * jnp.einsum("ihj,sjhe->sihe", logit_grad, key_rows, preferred_element_type=jnp.float32)
    ).astype(jnp.bfloat16)
    key_grad = (
        scale
        * jnp.einsum("ihj,sihe->sjhe", logit_grad, queries, preferred_element_type=jnp.float32)
    ).astype(jnp.bfloat16)
    value_grad = jnp.einsum(
        "ihj,sihe->sjhe", probs_low, attn_grad, preferred_element_type=jnp.float32
    ).astype(jnp.bfloat16)
    total = transposed_product(query_grad.reshape(-1, width), w_query)
    total = total + transposed_product(key_grad.reshape(-1, width), w_key)
    total = total + transposed_product(value_grad.reshape(-1, width), w_value)
    return total.reshape(seq_dev, length, width)


def solution(mesh):
    placed = (
        P(("grp", "seqa", "seqb"), None, None),
        P(("grp", "seqa", "seqb"), None, None),
        P(),
        P(),
        P(),
        P(),
        P("grp", None, None),
    )
    return jax.shard_map(
        local,
        mesh=mesh,
        in_specs=placed,
        out_specs=P(("grp", "seqa", "seqb"), None, None),
        check_vma=False,
    )
```

profile of v0, /device:TPU:0, one launch (start us, length us, event | category | flops | bytes accessed | tf_op | source)
XLA Modules:
  0.0 156.2 jit_solution(9128210285859536968)
XLA Ops:
  6.5 0.0 copy-start
  6.5 0.0 reduce-scatter.2.cloned.1.call-start
  6.5 1.4 copy-done
  7.9 3.8 %convolution_convert_fusion.3 = bf16[1024,768]{1,0:T(8,128)(2,1)} fusion(bf16[1024,768]{1,0:T(8,128)(2,1)S(1)} %bitcast.72, bf16[768,768]{1,0:T(8,128)(2,1)} %param.11), kind=kOutput, calls=%fused_computation.8 | convolution fusion | flops 1208745984 | bytes 4325376 | tf_op jit(solution)/shard_map/dot_general | solution.py:24
  11.7 1.7 %copy.33 = bf16[1024,768]{0,1:T(8,128)(2,1)S(1)} copy(bf16[1024,768]{1,0:T(8,128)(2,1)} %convolution_convert_fusion.3) | data formatting | bytes 3145728 | tf_op jit(solution)/shard_map/convert_element_type | solution.py:21
  13.5 2.4 %reshape.33 = bf16[4,256,12,64]{1,0,3,2:T(4,128)(2,1)} reshape(bf16[1024,768]{0,1:T(8,128)(2,1)S(1)} %copy.33) | data formatting | bytes 3145728 | tf_op jit(solution)/shard_map/reshape | solution.py:21
  15.8 4.3 %convolution_convert_fusion.2 = bf16[1024,768]{1,0:T(8,128)(2,1)} fusion(bf16[1024,768]{1,0:T(8,128)(2,1)} %bitcast.80, bf16[768,768]{1,0:T(8,128)(2,1)} %param.12), kind=kOutput, calls=%fused_computation.7 | convolution fusion | flops 1208745984 | bytes 4325376 | tf_op jit(solution)/shard_map/dot_general | solution.py:8
  20.1 1.7 %copy.34 = bf16[1024,768]{0,1:T(8,128)(2,1)S(1)} copy(bf16[1024,768]{1,0:T(8,128)(2,1)} %convolution_convert_fusion.2) | data formatting | bytes 3145728 | tf_op jit(solution)/shard_map/convert_element_type | solution.py:21
  21.9 2.4 %reshape.35 = bf16[4,256,12,64]{1,0,3,2:T(4,128)(2,1)} reshape(bf16[1024,768]{0,1:T(8,128)(2,1)S(1)} %copy.34) | data formatting | bytes 3145728 | tf_op jit(solution)/shard_map/reshape | solution.py:21
  24.2 2.6 %fusion.21 = bf16[256,12,256]{0,2,1:T(8,128)(2,1)S(1)} fusion(bf16[4,256,12,64]{1,0,3,2:T(4,128)(2,1)} %reshape.33, bf16[4,256,12,64]{1,0,3,2:T(4,128)(2,1)} %reshape.35), kind=kOutput, calls=%fused_computation.20 | convolution fusion | flops 403439616 | bytes 4718592 | tf_op jit(solution)/shard_map/sihe,sjhe->ihj/dot_general | solution.py:30
  26.8 3.0 %copy.37 = bf16[256,12,256]{2,1,0:T(8,128)(2,1)} copy(bf16[256,12,256]{0,2,1:T(8,128)(2,1)S(1)} %fusion.21) | data formatting | bytes 3145728 | tf_op jit(solution)/shard_map/convert_element_type | solution.py:30
  29.8 0.0 copy-start.5
  29.8 0.0 reduce-scatter.2.cloned.1.call-update
  29.8 0.0 all-gather.2.cloned.1.call-start
  29.9 1.0 constant_dynamic-slice_fusion
  30.9 63.6 %reduce-scatter.2.cloned.1.call-done = bf16[16,12,256]{2,1,0:T(8,128)(2,1)} async-done(((bf16[256,12,256]{2,1,0:T(8,128)(2,1)}), bf16[16,12,256]{2,1,0:T(8,128)(2,1)}) %reduce-scatter.2.cloned.1.call-update) | async-done | bytes 98320 | tf_op jit(solution)/shard_map/reduce_scatter | solution.py:29
  94.6 1.2 fusion.28
  95.8 0.7 copy.38
  96.4 0.0 all-gather.2.cloned.1.call-update
  96.5 0.0 copy-done.5
  96.5 2.5 %convolution_convert_fusion.1 = bf16[1024,768]{1,0:T(8,128)(2,1)} fusion(bf16[1024,768]{1,0:T(8,128)(2,1)S(1)} %bitcast.73, bf16[768,768]{1,0:T(8,128)(2,1)S(1)} %copy-done.5), kind=kOutput, calls=%fused_computation.6 | convolution fusion | flops 1208745984 | bytes 4325376 | tf_op jit(solution)/shard_map/dot_general | solution.py:26
  99.0 1.7 %copy.41 = bf16[1024,768]{0,1:T(8,128)(2,1)S(1)} copy(bf16[1024,768]{1,0:T(8,128)(2,1)} %convolution_convert_fusion.1) | data formatting | bytes 3145728 | tf_op jit(solution)/shard_map/convert_element_type | solution.py:21
  100.7 2.4 %reshape.37 = bf16[4,256,12,64]{1,0,3,2:T(4,128)(2,1)} reshape(bf16[1024,768]{0,1:T(8,128)(2,1)S(1)} %copy.41) | data formatting | bytes 3145728 | tf_op jit(solution)/shard_map/reshape | solution.py:21
  103.1 3.8 %convolution_convert_fusion.4 = bf16[1024,768]{1,0:T(8,128)(2,1)} fusion(bf16[1024,768]{1,0:T(8,128)(2,1)S(1)} %bitcast.71, bf16[768,768]{1,0:T(8,128)(2,1)} %param.10), kind=kOutput, calls=%fused_computation.9 | convolution fusion | flops 1208745984 | bytes 4325376 | tf_op jit(solution)/shard_map/dot_general | solution.py:27
  106.9 1.7 %copy.31 = bf16[1024,768]{0,1:T(8,128)(2,1)S(1)} copy(bf16[1024,768]{1,0:T(8,128)(2,1)} %convolution_convert_fusion.4) | data formatting | bytes 3145728 | tf_op jit(solution)/shard_map/convert_element_type | solution.py:21
  108.6 2.4 %reshape.32 = bf16[4,256,12,64]{1,0,3,2:T(4,128)(2,1)} reshape(bf16[1024,768]{0,1:T(8,128)(2,1)S(1)} %copy.31) | data formatting | bytes 3145728 | tf_op jit(solution)/shard_map/reshape | solution.py:21
  111.0 3.0 %fusion.8 = bf16[4,256,12,64]{1,3,0,2:T(8,128)(2,1)S(1)} fusion(f32[256,12,256]{2,0,1:T(8,128)} %param.13, bf16[4,256,12,64]{1,0,3,2:T(4,128)(2,1)} %reshape.35), kind=kOutput, calls=%fused_computation.17 | convolution fusion | flops 404226048 | bytes 6291456 | tf_op jit(solution)/shard_map/ihj,sihe->sjhe/dot_general | solution.py:52
  114.0 1.2 copy.45
  115.2 0.3 copy.52
  115.5 18.9 %all-gather.2.cloned.1.call-done = bf16[256,12,256]{2,0,1:T(8,128)(2,1)} async-done(((bf16[16,12,256]{2,0,1:T(8,128)(2,1)}), bf16[256,12,256]{2,0,1:T(8,128)(2,1)}) %all-gather.2.cloned.1.call-update) | async-done | bytes 1572880 | tf_op jit(solution)/shard_map/all_gather | solution.py:42
  134.4 2.5 %fusion.11 = bf16[4,256,12,64]{1,3,0,2:T(8,128)(2,1)S(1)} fusion(bf16[256,12,256]{2,0,1:T(8,128)(2,1)} %all-gather.2.cloned.1.call-done, bf16[4,256,12,64]{1,0,3,2:T(4,128)(2,1)} %reshape.32), kind=kOutput, calls=%fused_computation.18 | convolution fusion | flops 404226048 | bytes 4718592 | tf_op jit(solution)/shard_map/ihj,sjhe->sihe/dot_general | solution.py:46
  136.9 1.2 copy.40
  138.2 0.0 copy-start.1
  138.2 0.0 copy-start.3
  138.2 0.4 copy.50
  138.5 1.0 copy-done.1
  139.6 0.5 copy-done.3
  140.0 0.6 fusion.16
  140.6 1.2 copy.43
  141.8 0.0 copy-start.4
  141.9 0.3 copy.51
  142.2 0.9 copy-done.4
  143.1 1.5 fusion.32
  144.6 0.0 copy-done.6
  144.6 0.0 copy-start.2
  144.6 1.5 fusion.31
  146.1 0.0 copy-done.2
  146.1 3.2 %add_add_fusion = f32[1024,768]{1,0:T(8,128)} fusion(f32[1024,768]{1,0:T(8,128)S(1)} %fusion.31, f32[1024,768]{1,0:T(8,128)S(1)} %fusion.32, bf16[1024,768]{0,1:T(8,128)(2,1)S(1)} %bitcast.74, bf16[768,768]{1,0:T(8,128)(2,1)S(1)} %copy-done.2), kind=kOutput, calls=%fused_computation.2 | convolution fusion | flops 1209532416 | bytes 12189696 | tf_op jit(solution)/shard_map/dot_general | solution.py:8
  (1 shorter events, 0.0 us)
Async XLA Ops:
  6.5 1.4 copy-start
  6.5 88.0 %reduce-scatter.2.cloned.1.call-start = ((), (), s32[]{:S(2)}) async-start(), calls=%async_computation.1 | async-start | bytes 2228224 | tf_op jit(solution)/shard_map/reduce_scatter | solution.py:29
  29.8 66.7 %copy-start.5 = (bf16[768,768]{1,0:T(8,128)(2,1)S(1)}, bf16[768,768]{1,0:T(8,128)(2,1)}, u32[]{:S(2)}) copy-start(bf16[768,768]{1,0:T(8,128)(2,1)} %param.9) | copy-start | bytes 3538948
  29.8 104.6 %all-gather.2.cloned.1.call-start = ((), (), s32[]{:S(2)}) async-start(), calls=%async_computation.2 | async-start | bytes 1671168 | tf_op jit(solution)/shard_map/all_gather | solution.py:42
  138.2 1.4 copy-start.1
  138.2 1.9 %copy-start.3 = (bf16[256,12,256]{2,0,1:T(8,128)(2,1)S(1)}, bf16[256,12,256]{2,0,1:T(8,128)(2,1)}, u32[]{:S(2)}) copy-start(bf16[256,12,256]{2,0,1:T(8,128)(2,1)} %all-gather.2.cloned.1.call-done) | copy-start | bytes 4718596
  141.8 1.3 copy-start.4
  143.1 1.5 copy-start.6
  144.6 1.5 copy-start.2
Sparse Core Ops, SparseCore 0:
  30.0 64.5 reduce-scatter.1
  96.7 37.6 all-gather.1
where the time goes:
time: 157 us; the launch traced here: 156 us
  waiting for transfers between devices  82.6 us (53%)
  local copies, waits for them, and re-layouts  29.6 us (19%)
  matrix products  29.2 us (19%)
  between operations  13.6 us (9%)
    reduce_scatter x1, waiting for transfers between devices, local(): lax.psum_scatter(jnp.einsum('sihe,sjhe->ihj', attn_grad, values, preferre...  63.6 us
    all_gather x1, waiting for transfers between devices, local(): logit_grad = lax.all_gather(own_rows, ('seqa', 'seqb'), axis=0, tiled=True)  18.9 us
    dot_general x4, matrix products, transposed_product(): lax.dot_general(left, weight, (((1,), (1,)), ((), ())), preferred_element...  10.5 us
    reshape x4, local copies, waits for them, and re-layouts, shaped(): flat_rows.astype(jnp.bfloat16).reshape(seq_dev, length, heads, head_size)  9.48 us
    convert_element_type x4, local copies, waits for them, and re-layouts, shaped(): flat_rows.astype(jnp.bfloat16).reshape(seq_dev, length, heads, head_size)  6.84 us
    unnamed x17, local copies, waits for them, and re-layouts  4.88 us
    dot_general x1, matrix products, local(): jnp.dot(flat_in, w_key, preferred_element_type=jnp.float32)  3.81 us
    dot_general x1, matrix products, local(): jnp.dot(flat_in, w_value, preferred_element_type=jnp.float32)  3.8 us
  transfers between devices with their start and end apart: 2, of which 2 were waited for; matrix products, arithmetic and copies ran while one was open for 13% of the time, Pallas kernels for 0%

commit v1 on v0

v1 whole, which is shorter than its diff:
```python
import functools

import jax
import jax.numpy as jnp
from jax import lax
from jax.experimental import pallas as pl
from jax.experimental.pallas import tpu as pltpu
from jax.sharding import PartitionSpec as P


F32 = jnp.float32
BF16 = jnp.bfloat16
VMEM_LIMIT = 14 << 20
SEND_LIMIT = 14 << 20
GROUP = 4


def dot_nn(a, b):
    return lax.dot_general(a, b, (((1,), (0,)), ((), ())), preferred_element_type=F32)


def dot_nt(a, b):
    return lax.dot_general(a, b, (((1,), (1,)), ((), ())), preferred_element_type=F32)


def dot_tn(a, b):
    return lax.dot_general(a, b, (((0,), (0,)), ((), ())), preferred_element_type=F32)


def gather_head(rows, seqs, head, size):
    n = rows.shape[0] // seqs
    lanes = slice(head * size, (head + 1) * size)
    return jnp.concatenate([rows[s * n : (s + 1) * n, lanes] for s in range(seqs)], axis=1)


def spread_heads(parts, seqs, size):
    return [
        jnp.concatenate([p[:, s * size : (s + 1) * size] for p in parts], axis=1)
        for s in range(seqs)
    ]


def radices_of(count):
    out = []
    while count > 1:
        r = 4 if count % 4 == 0 else 2
        assert count % r == 0
        out.append(r)
        count //= r
    return tuple(out)


def position_of(mask, radices):
    pos, shift = 0, 0
    for r in radices:
        bits = r.bit_length() - 1
        pos = pos * r + ((mask >> shift) & (r - 1))
        shift += bits
    return pos


def fetch(pairs, sems):
    copies = [pltpu.make_async_copy(a, b, sems.at[i]) for i, (a, b) in enumerate(pairs)]
    for c in copies:
        c.start()
    return copies


def store_map(m, h, m_out, chip, others, rows, radices):
    for q in range(others):
        m_out[position_of(chip ^ q, radices), h] = m[q * rows : (q + 1) * rows]


def map_send_kernel(
    dims, radices, sc, x_hbm, wv_hbm, og_hbm, wo_hbm, m_out, a_out, v_out, x, og, wo, wv, sems
):
    seqs, length, heads, size, cores, others, rows = dims
    copies = fetch([(x_hbm, x), (wv_hbm, wv), (wo_hbm, wo), (og_hbm, og)], sems)
    width = x.shape[-1]
    half = length // cores
    start = pl.multiple_of((1 - sc[0]) * half, half)
    copies[0].wait()
    copies[1].wait()
    flat = x[...].reshape(seqs * length, width)
    for g in range(heads // GROUP):
        lanes = slice(g * GROUP * size, (g + 1) * GROUP * size)
        v4 = dot_nn(flat, wv[:, lanes]).astype(BF16)
        for h in range(GROUP):
            v_out[g * GROUP + h] = gather_head(v4, seqs, h, size)
    copies[2].wait()
    copies[3].wait()
    og_rows = og[:, pl.ds(start, half), :].reshape(seqs * half, width)
    for g in range(heads // GROUP):
        a4 = dot_nt(og_rows, wo[g * GROUP * size : (g + 1) * GROUP * size]).astype(BF16)
        for h in range(GROUP):
            a = gather_head(a4, seqs, h, size)
            a_out[g * GROUP + h] = a
            m = dot_nt(a, v_out[g * GROUP + h]).astype(BF16)
            store_map(m, g * GROUP + h, m_out, sc[1], others, rows, radices)


def map_keep_kernel(dims, radices, sc, og, wo, v_all, m_out, a_out):
    seqs, length, heads, size, cores, others, rows = dims
    width = og.shape[-1]
    half = length // cores
    start = pl.multiple_of(sc[0] * half, half)
    og_rows = og[:, pl.ds(start, half), :].reshape(seqs * half, width)
    for g in range(heads // GROUP):
        a4 = dot_nt(og_rows, wo[g * GROUP * size : (g + 1) * GROUP * size]).astype(BF16)
        for h in range(GROUP):
            a = gather_head(a4, seqs, h, size)
            a_out[g * GROUP + h] = a
            m = dot_nt(a, v_all[g * GROUP + h]).astype(BF16)
            store_map(m, g * GROUP + h, m_out, sc[1], others, rows, radices)


def value_kernel(dims, sc, a_own, a_other, wv, probs, o_out, p_out):
    seqs, length, heads, size, cores, _, rows = dims
    half = length // cores
    own = pl.multiple_of(sc[0] * half, half)
    other = pl.multiple_of((1 - sc[0]) * half, half)
    p_out[...] = probs[:, pl.ds(pl.multiple_of(own + sc[1] * rows, rows), rows), :]
    for g in range(heads // GROUP):
        lanes = slice(g * GROUP * size, (g + 1) * GROUP * size)
        parts = []
        for h in range(g * GROUP, (g + 1) * GROUP):
            p_own = probs[h, pl.ds(own, half), :].astype(BF16)
            p_other = probs[h, pl.ds(other, half), :].astype(BF16)
            vg = dot_tn(p_own, a_own[h]) + dot_tn(p_other, a_other[h])
            parts.append(vg.astype(BF16))
        for s, block in enumerate(spread_heads(parts, seqs, size)):
            term = dot_nt(block, wv[:, lanes])
            if g:
                o_out[s] += term
            else:
                o_out[s] = term


def query_key_kernel(dims, x, wq, wk, q_out, k_out):
    seqs, length, heads, size, _, _, _ = dims
    flat = x[...].reshape(seqs * length, x.shape[-1])
    for g in range(heads // GROUP):
        lanes = slice(g * GROUP * size, (g + 1) * GROUP * size)
        q4 = dot_nn(flat, wq[:, lanes]).astype(BF16)
        k4 = dot_nn(flat, wk[:, lanes]).astype(BF16)
        for h in range(GROUP):
            q_out[g * GROUP + h] = gather_head(q4, seqs, h, size)
            k_out[g * GROUP + h] = gather_head(k4, seqs, h, size)


def first_sum_kernel(radix, keep, recv, own_out, *outs):
    for m, out in zip(range(radix), (own_out,) + outs):
        total = keep[m].astype(F32) + recv[m].astype(F32)
        out[...] = total.astype(out.dtype)


def sum_kernel(radix, count, keep, *refs):
    terms, own_out, outs = refs[: count - 1], refs[count - 1], refs[count:]
    assert len(outs) == radix - 1
    for m, out in enumerate((own_out,) + outs):
        total = keep[m]
        for t in terms:
            total = total + t[m].astype(F32)
        out[...] = total.astype(out.dtype)


def softmax_kernel(p_rows, keep, *refs):
    terms, out = refs[:-1], refs[-1]
    total = keep[...]
    for t in terms:
        total = total + t[...].astype(F32)
    p = p_rows[...]
    inner = jnp.sum(p * total, axis=-1, keepdims=True)
    out[...] = (p * (total - inner)).astype(BF16)


def post_kernel(dims, radices, sc, *refs):
    seqs, length, heads, size, cores, others, rows = dims
    first = radices[0]
    own, other = refs[:first], refs[first : 2 * first]
    q_all, k_all, w_q, w_k, o_v, out_hbm, logit, q_grad, k_grad, out, sems = refs[2 * first :]
    scale = (size * seqs * cores * others) ** -0.5
    half = length // cores
    inner = others // first
    for which, parts in ((0, own), (1, other)):
        core = sc[0] if which == 0 else 1 - sc[0]
        for mask in range(others):
            pos = position_of(mask, radices)
            m, rest = pos // inner, pos % inner
            q = sc[1] ^ mask
            start = pl.multiple_of(core * half + q * rows, rows)
            for h in range(heads):
                logit[h, pl.ds(start, rows), :] = parts[m][rest, h]
    for g in range(heads // GROUP):
        qs, ks = [], []
        for h in range(g * GROUP, (g + 1) * GROUP):
            lg = logit[h]
            qs.append((scale * dot_nn(lg, k_all[h])).astype(BF16))
            ks.append((scale * dot_tn(lg, q_all[h])).astype(BF16))
        lanes = slice(g * GROUP * size, (g + 1) * GROUP * size)
        for s, block in enumerate(spread_heads(qs, seqs, size)):
            q_grad[s, :, lanes] = block
        for s, block in enumerate(spread_heads(ks, seqs, size)):
            k_grad[s, :, lanes] = block
    copies = []
    for s in range(seqs):
        out[s] = o_v[s] + dot_nt(q_grad[s], w_q[...]) + dot_nt(k_grad[s], w_k[...])
        copies.append(pltpu.make_async_copy(out.at[s], out_hbm.at[s], sems.at[s]))
        copies[-1].start()
    for c in copies:
        c.wait()


def exchange(x, axis, mask):
    count = lax.axis_size(axis)
    return lax.ppermute(x, axis, [(i, i ^ mask) for i in range(count)])


def cost(flops, nbytes):
    return pl.CostEstimate(flops=int(flops), bytes_accessed=int(nbytes), transcendentals=0)


def local(inputs, out_grad, w_query, w_key, w_value, w_output, saved_probs):
    seqs, length, width = inputs.shape
    heads = saved_probs.shape[1]
    size = width // heads
    cores, others = lax.axis_size("seqb"), lax.axis_size("seqa")
    rows = length // (cores * others)
    dims = (seqs, length, heads, size, cores, others, rows)
    radices = radices_of(others)
    half = length // cores
    lanes = seqs * size
    core, chip = lax.axis_index("seqb"), lax.axis_index("seqa")
    sc = jnp.stack([core, chip]).astype(jnp.int32)
    probs = jnp.swapaxes(saved_probs, 0, 1)
    params = pltpu.CompilerParams(vmem_limit_bytes=VMEM_LIMIT)
    proj = 2 * seqs * length * width * width
    mapf = 2 * heads * length * length * lanes
    smem = pl.BlockSpec(memory_space=pltpu.SMEM)
    vmem = pl.BlockSpec(memory_space=pltpu.VMEM)
    hbm = pl.BlockSpec(memory_space=pltpu.HBM)
    m_shape = jax.ShapeDtypeStruct((others, heads, rows, length), BF16)
    a_shape = jax.ShapeDtypeStruct((heads, half, lanes), BF16)
    v_shape = jax.ShapeDtypeStruct((heads, length, lanes), BF16)
    like = lambda a: jax.ShapeDtypeStruct(a.shape, a.dtype)

    m_send, a_other, v_all, x_in, og_in, wo_in, wv_in = pl.pallas_call(
        functools.partial(map_send_kernel, dims, radices),
        in_specs=[smem, hbm, hbm, hbm, hbm],
        out_specs=[vmem] * 7,
        out_shape=[m_shape, a_shape, v_shape, like(inputs), like(out_grad)]
        + [like(w_output), like(w_value)],
        scratch_shapes=[pltpu.SemaphoreType.DMA((4,))],
        compiler_params=pltpu.CompilerParams(vmem_limit_bytes=SEND_LIMIT),
        cost_estimate=cost(1.5 * proj + mapf / 2, 8e6),
        name="map_send",
    )(sc, *[pltpu.with_memory_space_constraint(a, pltpu.HBM) for a in (inputs, w_value, out_grad, w_output)])
    m_recv = exchange(m_send, "seqb", 1)
    m_keep, a_own = pl.pallas_call(
        functools.partial(map_keep_kernel, dims, radices),
        in_specs=[smem, vmem, vmem, vmem],
        out_specs=[vmem] * 2,
        out_shape=[m_shape, a_shape],
        compiler_params=params,
        cost_estimate=cost(0.5 * proj + mapf / 2, 5e6),
        name="map_keep",
    )(sc, og_in, wo_in, v_all)

    o_v, p_rows = pl.pallas_call(
        functools.partial(value_kernel, dims),
        in_specs=[smem] + [vmem] * 4,
        out_specs=[vmem] * 2,
        out_shape=[
            jax.ShapeDtypeStruct(inputs.shape, F32),
            jax.ShapeDtypeStruct((heads, rows, length), F32),
        ],
        compiler_params=params,
        cost_estimate=cost(proj + mapf, 8e6),
        name="value",
    )(sc, a_own, a_other, wv_in, probs)

    shape = lambda n: radices[n:] + (heads, rows, length)
    small = lambda kernel, outs: pl.pallas_call(
        kernel,
        out_specs=[vmem] * len(outs),
        out_shape=outs,
        compiler_params=pltpu.CompilerParams(vmem_limit_bytes=6 << 20),
        cost_estimate=cost(1e6, 1e6),
    )
    split = lambda n: [jax.ShapeDtypeStruct(shape(n + 1), F32)] + [
        jax.ShapeDtypeStruct(shape(n + 1), BF16)
    ] * (radices[n] - 1)
    keep, *sends = small(
        functools.partial(first_sum_kernel, radices[0]), split(0)
    )(m_keep.reshape(shape(0)), m_recv.reshape(shape(0)))
    shift = 0
    for n, r in enumerate(radices):
        terms = [exchange(x, "seqa", m << shift) for m, x in enumerate(sends, 1)]
        shift += r.bit_length() - 1
        if n + 1 < len(radices):
            keep, *sends = small(
                functools.partial(sum_kernel, radices[n + 1], r), split(n + 1)
            )(keep, *terms)
    (logit,) = small(
        softmax_kernel, [jax.ShapeDtypeStruct((heads, rows, length), BF16)]
    )(p_rows, keep, *terms)

    q_all, k_all = pl.pallas_call(
        functools.partial(query_key_kernel, dims),
        in_specs=[vmem] * 3,
        out_specs=[vmem] * 2,
        out_shape=[v_shape, v_shape],
        compiler_params=params,
        cost_estimate=cost(2 * proj, 6e6),
        name="query_key",
    )(x_in, w_query, w_key)

    parts = [logit]
    for n, r in list(enumerate(radices))[::-1]:
        block = jnp.stack(parts) if len(parts) > 1 else parts[0][None]
        if block.ndim > 4:
            block = block.reshape((-1,) + block.shape[2:])
        shift -= r.bit_length() - 1
        parts = [block] + [exchange(block, "seqa", m << shift) for m in range(1, r)]
    crossed = [exchange(p, "seqb", 1) for p in parts]

    return pl.pallas_call(
        functools.partial(post_kernel, dims, radices),
        in_specs=[smem] + [vmem] * (2 * radices[0] + 5),
        out_specs=hbm,
        scratch_shapes=[
            pltpu.VMEM((heads, length, length), BF16),
            pltpu.VMEM((seqs, length, width), BF16),
            pltpu.VMEM((seqs, length, width), BF16),
            pltpu.VMEM((seqs, length, width), F32),
            pltpu.SemaphoreType.DMA((seqs,)),
        ],
        out_shape=jax.ShapeDtypeStruct(inputs.shape, F32),
        compiler_params=params,
        cost_estimate=cost(2 * proj + 2 * mapf, 12e6),
        name="post",
    )(sc, *parts, *crossed, q_all, k_all, w_query, w_key, o_v)


def solution(mesh):
    placed = (
        P(("grp", "seqa", "seqb"), None, None),
        P(("grp", "seqa", "seqb"), None, None),
        P(),
        P(),
        P(),
        P(),
        P("grp", None, None),
    )

    return jax.shard_map(
        local,
        mesh=mesh,
        in_specs=placed,
        out_specs=P(("grp", "seqa", "seqb"), None, None),
        check_vma=False,
    )
```

time: 157 us -> 57 us (0.36)
  waiting for transfers between devices: 82.6 us -> 22.7 us
  local copies, waits for them, and re-layouts: 29.6 us -> 0.01 us
  matrix products: 29.2 us -> 0 us
  Pallas kernels: 0 us -> 21.5 us
  between operations: 13.6 us -> 0.1 us
  starting transfers between devices: 0.04 us -> 12.2 us
    reduce_scatter x1 -> x0, waiting for transfers between devices: 63.6 us -> none  [local(): lax.psum_scatter(jnp.einsum('sihe,sjhe->ihj', attn_grad, values, preferre...]
    dot_general x11 -> x0, matrix products: 29.2 us -> none  [the longest x4 10.5 us: transposed_product(): lax.dot_general(left, weight, (((1,), (1,)), ((), ())), preferred_element...]
    ppermute x0 -> x13, waiting for transfers between devices: none -> 22.7 us  [exchange(): return lax.ppermute(x, axis, [(i, i ^ mask) for i in range(count)])]
    pallas_call x0 -> x8, Pallas kernels: none -> 21.5 us  [the longest x1 6.8 us: local(): pl.pallas_call(functools.partial(map_send_kernel, dims, radices), in_spec...]
    all_gather x1 -> x0, waiting for transfers between devices: 18.9 us -> none  [local(): logit_grad = lax.all_gather(own_rows, ('seqa', 'seqb'), axis=0, tiled=True)]
    convert_element_type x9 -> x0, local copies, waits for them, and re-layouts: 14.2 us -> none  [the longest x4 6.84 us: shaped(): flat_rows.astype(jnp.bfloat16).reshape(seq_dev, length, heads, head_size)]
    ppermute x0 -> x13, starting transfers between devices: none -> 12.2 us  [exchange(): return lax.ppermute(x, axis, [(i, i ^ mask) for i in range(count)])]
    reshape x4 -> x0, local copies, waits for them, and re-layouts: 9.48 us -> none  [shaped(): flat_rows.astype(jnp.bfloat16).reshape(seq_dev, length, heads, head_size)]
  transfers between devices with their start and end apart: 2 -> 13, of which waited for: 2 -> 8; matrix products, arithmetic and copies ran while one was open for 13% -> 0% of each run, Pallas kernels for 0% -> 16%
where the time goes in v1:
time: 57 us; the launch traced here: 56.6 us
  waiting for transfers between devices  22.7 us (40%)
  Pallas kernels  21.5 us (38%)
  starting transfers between devices  12.2 us (21%)
    ppermute x13, waiting for transfers between devices, exchange(): return lax.ppermute(x, axis, [(i, i ^ mask) for i in range(count)])  22.7 us
    ppermute x13, starting transfers between devices, exchange(): return lax.ppermute(x, axis, [(i, i ^ mask) for i in range(count)])  12.2 us
    pallas_call x1, Pallas kernels, local(): pl.pallas_call(functools.partial(map_send_kernel, dims, radices), in_spec...  6.8 us
    pallas_call x1, Pallas kernels, local(): pl.pallas_call(functools.partial(post_kernel, dims, radices), in_specs=[s...  5.19 us
    pallas_call x1, Pallas kernels, local(): pl.pallas_call(functools.partial(value_kernel, dims), in_specs=[smem] + [...  3.3 us
    pallas_call x1, Pallas kernels, local(): pl.pallas_call(functools.partial(map_keep_kernel, dims, radices), in_spec...  3.13 us
    pallas_call x1, Pallas kernels, local(): pl.pallas_call(functools.partial(query_key_kernel, dims), in_specs=[vmem]...  2.72 us
  transfers between devices with their start and end apart: 13, of which 8 were waited for; matrix products, arithmetic and copies ran while one was open for 0% of the time, Pallas kernels for 16%

profile of v1, /device:TPU:0, one launch (start us, length us, event | category | flops | bytes accessed | tf_op | source)
XLA Modules:
  0.0 56.6 jit_solution(8194820820445294351)
XLA Ops:
  0.0 0.1 pad_add_fusion.sc
  0.1 6.8 %map_send.1 = (bf16[8,12,16,256]{3,2,1,0:T(8,128)(2,1)S(1)}, bf16[12,128,256]{2,1,0:T(8,128)(2,1)S(1)}, bf16[12,256,256]{2,1,0:T(8,128)(2,1)S(1)}, bf16[4,256,76...) custom-call(s32[2]{0:T(128)S(1)} %pad_add_fusion.sc, ...), custom_call_target="tpu_custom_call" | custom-call | flops 2013265920 | bytes 8000000 | tf_op jit(solution)/shard_map/map_send/pallas_call | solution.py:247
  6.9 0.6 collective-permute-start
  7.4 0.0 copy-start.2
  7.4 3.1 %map_keep.1 = (bf16[8,12,16,256]{3,2,1,0:T(8,128)(2,1)S(1)}, bf16[12,128,256]{2,1,0:T(8,128)(2,1)S(1)}) custom-call(s32[2]{0:T(128)S(1)} %pad_add_fusion.sc, bf16[4,256,768]{2,1,0:T(8,128)(2,1)S(1)} %get-tuple-element.24.og, bf16[768,768]{1,0:T(8,128)(2,1)S(1)} %get-tuple-element.25.wo, bf16[12,256,256]{2,1,0:T(8,128)(2,1)S(1)} %get-tuple-element.26.v_all), custom_call_target="tpu_custom_call" | custom-call | flops 805306368 | bytes 5000000 | tf_op jit(solution)/shard_map/map_keep/pallas_call | solution.py:259
  10.6 0.0 collective-permute-done
  10.6 0.2 shard_map.73
  10.8 2.6 %collective-permute-start.1 = (bf16[2,12,16,256]{3,2,1,0:T(8,128)(2,1)S(1)}, bf16[2,12,16,256]{3,2,1,0:T(8,128)(2,1)S(1)}, u32[]{:S(2)}, u32[]{:S(2)}) collective-permute-start(bf16[2,12,16,256]{3,2,1,0:T(8,128)(2,1)S(1)} %get-tuple-element.34), channel_id=1, source_target_pairs={{0,2},{2,0},{4,6},{6,4},{8,10},{10,8},{12,14},{14,12},{1,3},{3,1},... | collective-permute-start | bytes 589832 | tf_op jit(solution)/shard_map/ppermute | solution.py:216
  13.4 1.6 %collective-permute-start.2 = (bf16[2,12,16,256]{3,2,1,0:T(8,128)(2,1)S(1)}, bf16[2,12,16,256]{3,2,1,0:T(8,128)(2,1)S(1)}, u32[]{:S(2)}, u32[]{:S(2)}) collective-permute-start(bf16[2,12,16,256]{3,2,1,0:T(8,128)(2,1)S(1)} %get-tuple-element.35), channel_id=1, source_target_pairs={{0,4},{2,6},{4,0},{6,2},{8,12},{10,14},{12,8},{14,10},{1,5},{3,7},... | collective-permute-start | bytes 589832 | tf_op jit(solution)/shard_map/ppermute | solution.py:216
  14.9 0.0 collective-permute-start.3
  15.0 4.0 %collective-permute-done.1.refs_0_ = bf16[2,12,16,256]{3,2,1,0:T(8,128)(2,1)S(1)} collective-permute-done((bf16[2,12,16,256]{3,2,1,0:T(8,128)(2,1)S(1)}, bf16[2,12,16,256]{3,2,1,0:T(8,128)(2,1)S(1)}, u32[]{:S(2)}, u32[]{:S(2)}) %collective-permute-start.1) | collective-permute-done | bytes 196640 | tf_op jit(solution)/shard_map/ppermute | solution.py:216
  18.9 2.2 %collective-permute-done.2.refs_1_ = bf16[2,12,16,256]{3,2,1,0:T(8,128)(2,1)S(1)} collective-permute-done((bf16[2,12,16,256]{3,2,1,0:T(8,128)(2,1)S(1)}, bf16[2,12,16,256]{3,2,1,0:T(8,128)(2,1)S(1)}, u32[]{:S(2)}, u32[]{:S(2)}) %collective-permute-start.2) | collective-permute-done | bytes 196640 | tf_op jit(solution)/shard_map/ppermute | solution.py:216
  21.1 3.2 %collective-permute-done.3.refs_2_ = bf16[2,12,16,256]{3,2,1,0:T(8,128)(2,1)S(1)} collective-permute-done((bf16[2,12,16,256]{3,2,1,0:T(8,128)(2,1)S(1)}, bf16[2,12,16,256]{3,2,1,0:T(8,128)(2,1)S(1)}, u32[]{:S(2)}, u32[]{:S(2)}) %collective-permute-start.3) | collective-permute-done | bytes 196640 | tf_op jit(solution)/shard_map/ppermute | solution.py:216
  24.4 0.1 shard_map.74
  24.5 2.8 %collective-permute-start.4 = (bf16[12,16,256]{2,1,0:T(8,128)(2,1)S(1)}, bf16[12,16,256]{2,1,0:T(8,128)(2,1)S(1)}, u32[]{:S(2)}, u32[]{:S(2)}) collective-permute-start(bf16[12,16,256]{2,1,0:T(8,128)(2,1)S(1)} %get-tuple-element.38), channel_id=1, source_target_pairs={{0,8},{2,10},{4,12},{6,14},{8,0},{10,2},{12,4},{14,6},{1,9},{3,11}... | collective-permute-start | bytes 294920 | tf_op jit(solution)/shard_map/ppermute | solution.py:216
  27.3 0.0 copy-done.2
  27.3 0.0 copy-start
  27.3 0.0 copy-start.1
  27.3 3.3 %value.1 = (f32[4,256,768]{2,1,0:T(8,128)S(1)}, f32[12,16,256]{2,1,0:T(8,128)S(1)}) custom-call(s32[2]{0:T(128)S(1)} %pad_add_fusion.sc, bf16[12,128,256]{2,1,0:T(8,128)(2,1)S(1)} %get-tuple-element.27.a_own, bf16[12,128,256]{2,1,0:T(8,128)(2,1)S(1)} %get-tuple-element.28.a_other, bf16[768,768]{1,0:T(8,128)(2,1)S(1)} %get-tuple-element.29.wv, ...), custom_call_target="tpu_custom_call" | custom-call | flops 1610612736 | bytes 8000000 | tf_op jit(solution)/shard_map/value/pallas_call | solution.py:269
  30.6 1.3 %collective-permute-done.4.refs_0_ = bf16[12,16,256]{2,1,0:T(8,128)(2,1)S(1)} collective-permute-done((bf16[12,16,256]{2,1,0:T(8,128)(2,1)S(1)}, bf16[12,16,256]{2,1,0:T(8,128)(2,1)S(1)}, u32[]{:S(2)}, u32[]{:S(2)}) %collective-permute-start.4) | collective-permute-done | bytes 98336 | tf_op jit(solution)/shard_map/ppermute | solution.py:216
  31.9 0.1 shard_map.75
  32.0 1.1 %collective-permute-start.5 = (bf16[1,12,16,256]{3,2,1,0:T(8,128)(2,1)S(1)}, bf16[1,12,16,256]{3,2,1,0:T(8,128)(2,1)S(1)}, u32[]{:S(2)}, u32[]{:S(2)}) collective-permute-start(bf16[1,12,16,256]{3,2,1,0:T(8,128)(2,1)S(1)} %bitcast.12), channel_id=1, source_target_pairs={{0,8},{2,10},{4,12},{6,14},{8,0},{10,2},{12,4},{14,6},{1,9},{3,11}... | collective-permute-start | bytes 294920 | tf_op jit(solution)/shard_map/ppermute | solution.py:216
  33.1 5.8 %collective-permute-done.5 = bf16[1,12,16,256]{3,2,1,0:T(8,128)(2,1)S(1)} collective-permute-done((bf16[1,12,16,256]{3,2,1,0:T(8,128)(2,1)S(1)}, bf16[1,12,16,256]{3,2,1,0:T(8,128)(2,1)S(1)}, u32[]{:S(2)}, u32[]{:S(2)}) %collective-permute-start.5) | collective-permute-done | bytes 98336 | tf_op jit(solution)/shard_map/ppermute | solution.py:216
  38.9 0.8 %collective-permute-start.8 = (bf16[2,12,16,256]{3,2,1,0:T(8,128)(2,1)S(1)}, bf16[2,12,16,256]{3,2,1,0:T(8,128)(2,1)S(1)}, u32[]{:S(2)}, u32[]{:S(2)}) collective-permute-start(bf16[2,12,16,256]{3,2,1,0:T(8,128)(2,1)S(1)} %maximum_bitcast_fusion.refs_0_), channel_id=1, source_target_pairs={{0,6},{2,4},{4,2},{6,0},{8,14},{10,12},{12,10},{14,8},{1,7},{3,5},... | collective-permute-start | bytes 589832 | tf_op jit(solution)/shard_map/ppermute | solution.py:216
  39.7 2.2 %collective-permute-start.7 = (bf16[2,12,16,256]{3,2,1,0:T(8,128)(2,1)S(1)}, bf16[2,12,16,256]{3,2,1,0:T(8,128)(2,1)S(1)}, u32[]{:S(2)}, u32[]{:S(2)}) collective-permute-start(bf16[2,12,16,256]{3,2,1,0:T(8,128)(2,1)S(1)} %maximum_bitcast_fusion.refs_0_), channel_id=1, source_target_pairs={{0,4},{2,6},{4,0},{6,2},{8,12},{10,14},{12,8},{14,10},{1,5},{3,7},... | collective-permute-start | bytes 589832 | tf_op jit(solution)/shard_map/ppermute | solution.py:216
  41.9 0.5 collective-permute-start.6
  42.4 0.0 collective-permute-start.9
  42.4 4.2 %collective-permute-done.8.refs_3_ = bf16[2,12,16,256]{3,2,1,0:T(8,128)(2,1)S(1)} collective-permute-done((bf16[2,12,16,256]{3,2,1,0:T(8,128)(2,1)S(1)}, bf16[2,12,16,256]{3,2,1,0:T(8,128)(2,1)S(1)}, u32[]{:S(2)}, u32[]{:S(2)}) %collective-permute-start.8) | collective-permute-done | bytes 196640 | tf_op jit(solution)/shard_map/ppermute | solution.py:216
  46.6 0.0 collective-permute-start.12
  46.7 1.4 %collective-permute-done.7.refs_2_ = bf16[2,12,16,256]{3,2,1,0:T(8,128)(2,1)S(1)} collective-permute-done((bf16[2,12,16,256]{3,2,1,0:T(8,128)(2,1)S(1)}, bf16[2,12,16,256]{3,2,1,0:T(8,128)(2,1)S(1)}, u32[]{:S(2)}, u32[]{:S(2)}) %collective-permute-start.7) | collective-permute-done | bytes 196640 | tf_op jit(solution)/shard_map/ppermute | solution.py:216
  48.0 0.0 collective-permute-start.11
  48.0 0.6 %collective-permute-done.6.refs_1_ = bf16[2,12,16,256]{3,2,1,0:T(8,128)(2,1)S(1)} collective-permute-done((bf16[2,12,16,256]{3,2,1,0:T(8,128)(2,1)S(1)}, bf16[2,12,16,256]{3,2,1,0:T(8,128)(2,1)S(1)}, u32[]{:S(2)}, u32[]{:S(2)}) %collective-permute-start.6) | collective-permute-done | bytes 196640 | tf_op jit(solution)/shard_map/ppermute | solution.py:216
  48.7 0.0 collective-permute-start.10
  48.7 0.0 copy-done
  48.7 0.0 copy-done.1
  48.7 2.7 %query_key.1 = (bf16[12,256,256]{2,1,0:T(8,128)(2,1)S(1)}, bf16[12,256,256]{2,1,0:T(8,128)(2,1)S(1)}) custom-call(bf16[4,256,768]{2,1,0:T(8,128)(2,1)S(1)} %get-tuple-element.39.x, bf16[768,768]{1,0:T(8,128)(2,1)S(1)} %copy-done, bf16[768,768]{1,0:T(8,128)(2,1)S(1)} %copy-done.1), custom_call_target="tpu_custom_call" | custom-call | flops 2415919104 | bytes 6000000 | tf_op jit(solution)/shard_map/query_key/pallas_call | solution.py:308
  51.4 0.0 collective-permute-done.9.refs_4_
  51.4 0.0 collective-permute-done.12.refs_7_
  51.4 0.0 collective-permute-done.11.refs_6_
  51.4 0.0 collective-permute-done.10.refs_5_
  51.4 5.2 %post.1 = f32[4,256,768]{2,1,0:T(8,128)} custom-call(s32[2]{0:T(128)S(1)} %pad_add_fusion.sc, bf16[2,12,16,256]{3,2,1,0:T(8,128)(2,1)S(1)} %maximum_bitcast_fusion.refs_0_, bf16[2,12,16,256]{3,2,1,0:T(8,128)(2,1)S(1)} %collective-permute-done.6.refs_1_, bf16[2,12,16,256]{3,2,1,0:T(8,128)(2,1)S(1)} %collective-permute-done.7.refs_2_, ...), custom_call_target="tpu_custom_call" | custom-call | flops 3221225472 | bytes 12000000 | tf_op jit(solution)/shard_map/post/pallas_call | solution.py:327
  (1 shorter events, 0.0 us)
Async XLA Ops:
  6.9 3.7 %collective-permute-start = (bf16[8,12,16,256]{3,2,1,0:T(8,128)(2,1)S(1)}, bf16[8,12,16,256]{3,2,1,0:T(8,128)(2,1)S(1)}, u32[]{:S(2)}, u32[]{:S(2)}) collective-permute-start(bf16[8,12,16,256]{3,2,1,0:T(8,128)(2,1)S(1)} %get-tuple-element.32), channel_id=1, source_target_pairs={{0,1},{1,0},{2,3},{3,2},{4,5},{5,4},{6,7},{7,6},{8,9},{9,8},{10,11... | collective-permute-start | bytes 2359304 | tf_op jit(solution)/shard_map/ppermute | solution.py:216
  7.4 19.8 %copy-start.2 = (f32[256,12,256]{2,0,1:T(8,128)S(1)}, f32[256,12,256]{2,0,1:T(8,128)}, u32[]{:S(2)}) copy-start(f32[256,12,256]{2,0,1:T(8,128)} %param.13) | copy-start | bytes 9437188
  10.8 8.1 %collective-permute-start.1 = (bf16[2,12,16,256]{3,2,1,0:T(8,128)(2,1)S(1)}, bf16[2,12,16,256]{3,2,1,0:T(8,128)(2,1)S(1)}, u32[]{:S(2)}, u32[]{:S(2)}) collective-permute-start(bf16[2,12,16,256]{3,2,1,0:T(8,128)(2,1)S(1)} %get-tuple-element.34), channel_id=1, source_target_pairs={{0,2},{2,0},{4,6},{6,4},{8,10},{10,8},{12,14},{14,12},{1,3},{3,1},... | collective-permute-start | bytes 589832 | tf_op jit(solution)/shard_map/ppermute | solution.py:216
  13.4 7.8 %collective-permute-start.2 = (bf16[2,12,16,256]{3,2,1,0:T(8,128)(2,1)S(1)}, bf16[2,12,16,256]{3,2,1,0:T(8,128)(2,1)S(1)}, u32[]{:S(2)}, u32[]{:S(2)}) collective-permute-start(bf16[2,12,16,256]{3,2,1,0:T(8,128)(2,1)S(1)} %get-tuple-element.35), channel_id=1, source_target_pairs={{0,4},{2,6},{4,0},{6,2},{8,12},{10,14},{12,8},{14,10},{1,5},{3,7},... | collective-permute-start | bytes 589832 | tf_op jit(solution)/shard_map/ppermute | solution.py:216
  14.9 9.4 %collective-permute-start.3 = (bf16[2,12,16,256]{3,2,1,0:T(8,128)(2,1)S(1)}, bf16[2,12,16,256]{3,2,1,0:T(8,128)(2,1)S(1)}, u32[]{:S(2)}, u32[]{:S(2)}) collective-permute-start(bf16[2,12,16,256]{3,2,1,0:T(8,128)(2,1)S(1)} %get-tuple-element.36), channel_id=1, source_target_pairs={{0,6},{2,4},{4,2},{6,0},{8,14},{10,12},{12,10},{14,8},{1,7},{3,5},... | collective-permute-start | bytes 589832 | tf_op jit(solution)/shard_map/ppermute | solution.py:216
  24.5 7.4 %collective-permute-start.4 = (bf16[12,16,256]{2,1,0:T(8,128)(2,1)S(1)}, bf16[12,16,256]{2,1,0:T(8,128)(2,1)S(1)}, u32[]{:S(2)}, u32[]{:S(2)}) collective-permute-start(bf16[12,16,256]{2,1,0:T(8,128)(2,1)S(1)} %get-tuple-element.38), channel_id=1, source_target_pairs={{0,8},{2,10},{4,12},{6,14},{8,0},{10,2},{12,4},{14,6},{1,9},{3,11}... | collective-permute-start | bytes 294920 | tf_op jit(solution)/shard_map/ppermute | solution.py:216
  27.3 21.4 %copy-start = (bf16[768,768]{1,0:T(8,128)(2,1)S(1)}, bf16[768,768]{1,0:T(8,128)(2,1)}, u32[]{:S(2)}) copy-start(bf16[768,768]{1,0:T(8,128)(2,1)} %refs_10_.1) | copy-start | bytes 3538948
  27.3 21.4 %copy-start.1 = (bf16[768,768]{1,0:T(8,128)(2,1)S(1)}, bf16[768,768]{1,0:T(8,128)(2,1)}, u32[]{:S(2)}) copy-start(bf16[768,768]{1,0:T(8,128)(2,1)} %refs_11_.1) | copy-start | bytes 3538948
  32.0 6.9 %collective-permute-start.5 = (bf16[1,12,16,256]{3,2,1,0:T(8,128)(2,1)S(1)}, bf16[1,12,16,256]{3,2,1,0:T(8,128)(2,1)S(1)}, u32[]{:S(2)}, u32[]{:S(2)}) collective-permute-start(bf16[1,12,16,256]{3,2,1,0:T(8,128)(2,1)S(1)} %bitcast.12), channel_id=1, source_target_pairs={{0,8},{2,10},{4,12},{6,14},{8,0},{10,2},{12,4},{14,6},{1,9},{3,11}... | collective-permute-start | bytes 294920 | tf_op jit(solution)/shard_map/ppermute | solution.py:216
  38.9 7.8 %collective-permute-start.8 = (bf16[2,12,16,256]{3,2,1,0:T(8,128)(2,1)S(1)}, bf16[2,12,16,256]{3,2,1,0:T(8,128)(2,1)S(1)}, u32[]{:S(2)}, u32[]{:S(2)}) collective-permute-start(bf16[2,12,16,256]{3,2,1,0:T(8,128)(2,1)S(1)} %maximum_bitcast_fusion.refs_0_), channel_id=1, source_target_pairs={{0,6},{2,4},{4,2},{6,0},{8,14},{10,12},{12,10},{14,8},{1,7},{3,5},... | collective-permute-start | bytes 589832 | tf_op jit(solution)/shard_map/ppermute | solution.py:216
  39.7 8.3 %collective-permute-start.7 = (bf16[2,12,16,256]{3,2,1,0:T(8,128)(2,1)S(1)}, bf16[2,12,16,256]{3,2,1,0:T(8,128)(2,1)S(1)}, u32[]{:S(2)}, u32[]{:S(2)}) collective-permute-start(bf16[2,12,16,256]{3,2,1,0:T(8,128)(2,1)S(1)} %maximum_bitcast_fusion.refs_0_), channel_id=1, source_target_pairs={{0,4},{2,6},{4,0},{6,2},{8,12},{10,14},{12,8},{14,10},{1,5},{3,7},... | collective-permute-start | bytes 589832 | tf_op jit(solution)/shard_map/ppermute | solution.py:216
  41.9 6.7 %collective-permute-start.6 = (bf16[2,12,16,256]{3,2,1,0:T(8,128)(2,1)S(1)}, bf16[2,12,16,256]{3,2,1,0:T(8,128)(2,1)S(1)}, u32[]{:S(2)}, u32[]{:S(2)}) collective-permute-start(bf16[2,12,16,256]{3,2,1,0:T(8,128)(2,1)S(1)} %maximum_bitcast_fusion.refs_0_), channel_id=1, source_target_pairs={{0,2},{2,0},{4,6},{6,4},{8,10},{10,8},{12,14},{14,12},{1,3},{3,1},... | collective-permute-start | bytes 589832 | tf_op jit(solution)/shard_map/ppermute | solution.py:216
  42.4 9.0 %collective-permute-start.9 = (bf16[2,12,16,256]{3,2,1,0:T(8,128)(2,1)S(1)}, bf16[2,12,16,256]{3,2,1,0:T(8,128)(2,1)S(1)}, u32[]{:S(2)}, u32[]{:S(2)}) collective-permute-start(bf16[2,12,16,256]{3,2,1,0:T(8,128)(2,1)S(1)} %maximum_bitcast_fusion.refs_0_), channel_id=1, source_target_pairs={{0,1},{1,0},{2,3},{3,2},{4,5},{5,4},{6,7},{7,6},{8,9},{9,8},{10,11... | collective-permute-start | bytes 589832 | tf_op jit(solution)/shard_map/ppermute | solution.py:216
  46.6 4.8 %collective-permute-start.12 = (bf16[2,12,16,256]{3,2,1,0:T(8,128)(2,1)S(1)}, bf16[2,12,16,256]{3,2,1,0:T(8,128)(2,1)S(1)}, u32[]{:S(2)}, u32[]{:S(2)}) collective-permute-start(bf16[2,12,16,256]{3,2,1,0:T(8,128)(2,1)S(1)} %collective-permute-done.8.refs_3_), channel_id=1, source_target_pairs={{0,1},{1,0},{2,3},{3,2},{4,5},{5,4},{6,7},{7,6},{8,9},{9,8},{10,11... | collective-permute-start | bytes 589832 | tf_op jit(solution)/shard_map/ppermute | solution.py:216
  48.0 3.4 %collective-permute-start.11 = (bf16[2,12,16,256]{3,2,1,0:T(8,128)(2,1)S(1)}, bf16[2,12,16,256]{3,2,1,0:T(8,128)(2,1)S(1)}, u32[]{:S(2)}, u32[]{:S(2)}) collective-permute-start(bf16[2,12,16,256]{3,2,1,0:T(8,128)(2,1)S(1)} %collective-permute-done.7.refs_2_), channel_id=1, source_target_pairs={{0,1},{1,0},{2,3},{3,2},{4,5},{5,4},{6,7},{7,6},{8,9},{9,8},{10,11... | collective-permute-start | bytes 589832 | tf_op jit(solution)/shard_map/ppermute | solution.py:216
  48.7 2.8 %collective-permute-start.10 = (bf16[2,12,16,256]{3,2,1,0:T(8,128)(2,1)S(1)}, bf16[2,12,16,256]{3,2,1,0:T(8,128)(2,1)S(1)}, u32[]{:S(2)}, u32[]{:S(2)}) collective-permute-start(bf16[2,12,16,256]{3,2,1,0:T(8,128)(2,1)S(1)} %collective-permute-done.6.refs_1_), channel_id=1, source_target_pairs={{0,1},{1,0},{2,3},{3,2},{4,5},{5,4},{6,7},{7,6},{8,9},{9,8},{10,11... | collective-permute-start | bytes 589832 | tf_op jit(solution)/shard_map/ppermute | solution.py:216

commit v2 on v1

v2 whole, which is shorter than its diff:
```python
import functools

import jax
import jax.numpy as jnp
from jax import lax
from jax.experimental import pallas as pl
from jax.experimental.pallas import tpu as pltpu
from jax.sharding import PartitionSpec as P


F32 = jnp.float32
BF16 = jnp.bfloat16
VMEM_LIMIT = 14 << 20
FIRST_PART = 0.67
GROUP = 4


def dot_nn(a, b):
    return lax.dot_general(a, b, (((1,), (0,)), ((), ())), preferred_element_type=F32)


def dot_nt(a, b):
    return lax.dot_general(a, b, (((1,), (1,)), ((), ())), preferred_element_type=F32)


def dot_tn(a, b):
    return lax.dot_general(a, b, (((0,), (0,)), ((), ())), preferred_element_type=F32)


def gather_head(rows, seqs, head, size):
    n = rows.shape[0] // seqs
    lanes = slice(head * size, (head + 1) * size)
    return jnp.concatenate([rows[s * n : (s + 1) * n, lanes] for s in range(seqs)], axis=1)


def spread_heads(parts, seqs, size):
    return [
        jnp.concatenate([p[:, s * size : (s + 1) * size] for p in parts], axis=1)
        for s in range(seqs)
    ]


def radices_of(count):
    out = []
    while count > 1:
        r = 4 if count % 4 == 0 else 2
        assert count % r == 0
        out.append(r)
        count //= r
    return tuple(out)


def position_of(mask, radices):
    pos, shift = 0, 0
    for r in radices:
        bits = r.bit_length() - 1
        pos = pos * r + ((mask >> shift) & (r - 1))
        shift += bits
    return pos


def fetch(pairs, sems):
    copies = [pltpu.make_async_copy(a, b, sems.at[i]) for i, (a, b) in enumerate(pairs)]
    for c in copies:
        c.start()
    return copies


def store_map(m, h, m_out, chip, others, rows, radices):
    for q in range(others):
        m_out[position_of(chip ^ q, radices), h] = m[q * rows : (q + 1) * rows]


def groups_of(count):
    return [(g, min(g + GROUP, count)) for g in range(0, count, GROUP)]


def value_rows(x, wv, v_out, first, dims):
    seqs, length, _, size, _, _, _ = dims
    flat = x[...].reshape(seqs * length, x.shape[-1])
    for a, b in groups_of(v_out.shape[0]):
        v4 = dot_nn(flat, wv[:, (first + a) * size : (first + b) * size]).astype(BF16)
        for h in range(b - a):
            v_out[a + h] = gather_head(v4, seqs, h, size)


def attn_rows(og, wo, a_out, first, dims):
    seqs, length, _, size, _, _, _ = dims
    flat = og[...].reshape(seqs * length, og.shape[-1])
    for a, b in groups_of(a_out.shape[0]):
        a4 = dot_nt(flat, wo[(first + a) * size : (first + b) * size]).astype(BF16)
        for h in range(b - a):
            a_out[a + h] = gather_head(a4, seqs, h, size)


def map_rows(core, chip, a_all, v_all, m_out, dims, radices):
    _, length, _, _, cores, others, rows = dims
    half = length // cores
    start = pl.multiple_of(core * half, half)
    for h in range(v_all.shape[0]):
        m = dot_nt(a_all[h, pl.ds(start, half), :], v_all[h]).astype(BF16)
        store_map(m, h, m_out, chip, others, rows, radices)


def first_map_kernel(
    dims, radices, sc, x_hbm, wv_hbm, og_hbm, wo_hbm, m_out, a_out, v_out, x, og, wo, wv, sems
):
    copies = fetch([(x_hbm, x), (wv_hbm, wv), (wo_hbm, wo), (og_hbm, og)], sems)
    copies[0].wait()
    copies[1].wait()
    value_rows(x, wv, v_out, 0, dims)
    copies[2].wait()
    copies[3].wait()
    attn_rows(og, wo, a_out, 0, dims)
    map_rows(1 - sc[0], sc[1], a_out, v_out, m_out, dims, radices)


def map_send_kernel(dims, radices, first, sc, x, wv, og, wo, m_out, a_out, v_out):
    value_rows(x, wv, v_out, first, dims)
    attn_rows(og, wo, a_out, first, dims)
    map_rows(1 - sc[0], sc[1], a_out, v_out, m_out, dims, radices)


def map_keep_kernel(dims, radices, sc, a_all, v_all, m_out):
    map_rows(sc[0], sc[1], a_all, v_all, m_out, dims, radices)


def value_kernel(dims, chunks, sc, *refs):
    seqs, length, _, size, _, others, rows = dims
    a_refs, (wv, probs, o_out), p_outs = (
        refs[: len(chunks)],
        refs[len(chunks) : len(chunks) + 3],
        refs[len(chunks) + 3 : -1],
    )
    v_grad = refs[-1]
    mine = pl.ds(pl.multiple_of((sc[0] * others + sc[1]) * rows, rows), rows)
    for (first, n), a_all, p_out in zip(chunks, a_refs, p_outs):
        p_out[...] = probs[first : first + n, mine, :]
        for a, b in groups_of(n):
            parts = [
                dot_tn(probs[first + h].astype(BF16), a_all[h]).astype(BF16)
                for h in range(a, b)
            ]
            lanes = slice((first + a) * size, (first + b) * size)
            for s, block in enumerate(spread_heads(parts, seqs, size)):
                v_grad[s * length : (s + 1) * length, lanes] = block
    o_out[...] = dot_nt(v_grad[...], wv[...]).reshape(o_out.shape)


def query_key_kernel(dims, x, wq, wk, q_out, k_out):
    seqs, length, heads, size, _, _, _ = dims
    flat = x[...].reshape(seqs * length, x.shape[-1])
    for g in range(heads // GROUP):
        lanes = slice(g * GROUP * size, (g + 1) * GROUP * size)
        q4 = dot_nn(flat, wq[:, lanes]).astype(BF16)
        k4 = dot_nn(flat, wk[:, lanes]).astype(BF16)
        for h in range(GROUP):
            q_out[g * GROUP + h] = gather_head(q4, seqs, h, size)
            k_out[g * GROUP + h] = gather_head(k4, seqs, h, size)


def first_sum_kernel(radix, keep, recv, own_out, *outs):
    for m, out in zip(range(radix), (own_out,) + outs):
        total = keep[m].astype(F32) + recv[m].astype(F32)
        out[...] = total.astype(out.dtype)


def sum_kernel(radix, count, keep, *refs):
    terms, own_out, outs = refs[: count - 1], refs[count - 1], refs[count:]
    assert len(outs) == radix - 1
    for m, out in enumerate((own_out,) + outs):
        total = keep[m]
        for t in terms:
            total = total + t[m].astype(F32)
        out[...] = total.astype(out.dtype)


def softmax_kernel(p_rows, keep, *refs):
    terms, out = refs[:-1], refs[-1]
    total = keep[...]
    for t in terms:
        total = total + t[...].astype(F32)
    p = p_rows[...]
    inner = jnp.sum(p * total, axis=-1, keepdims=True)
    out[...] = (p * (total - inner)).astype(BF16)


def post_kernel(dims, radices, chunk, last, sc, *refs):
    seqs, length, _, size, cores, others, rows = dims
    first_head, count = chunk
    first = radices[0]
    own, other = refs[:first], refs[first : 2 * first]
    q_all, k_all, w_q, w_k, o_in, out, logit, grads = refs[2 * first : 2 * first + 8]
    scale = (size * seqs * cores * others) ** -0.5
    half = length // cores
    inner = others // first
    for which, parts in ((0, own), (1, other)):
        core = sc[0] if which == 0 else 1 - sc[0]
        for mask in range(others):
            pos = position_of(mask, radices)
            m, rest = pos // inner, pos % inner
            q = sc[1] ^ mask
            start = pl.multiple_of(core * half + q * rows, rows)
            for h in range(count):
                logit[h, pl.ds(start, rows), :] = parts[m][rest, h]
    width = count * size
    for a, b in groups_of(count):
        qs, ks = [], []
        for h in range(a, b):
            lg = logit[h]
            qs.append((scale * dot_nn(lg, k_all[first_head + h])).astype(BF16))
            ks.append((scale * dot_tn(lg, q_all[first_head + h])).astype(BF16))
        for at, parts in ((0, qs), (width, ks)):
            for s, block in enumerate(spread_heads(parts, seqs, size)):
                grads[s * length : (s + 1) * length, at + a * size : at + b * size] = block
    lanes = slice(first_head * size, (first_head + count) * size)
    weights = jnp.concatenate([w_q[:, lanes], w_k[:, lanes]], axis=1)
    if not last:
        out[...] = o_in[...] + dot_nt(grads[...], weights).reshape(out.shape)
        return
    staged, sems = refs[-2:]
    copies = []
    for s in range(seqs):
        staged[s] = o_in[s] + dot_nt(grads[s * length : (s + 1) * length], weights)
        copies.append(pltpu.make_async_copy(staged.at[s], out.at[s], sems.at[s]))
        copies[-1].start()
    for c in copies:
        c.wait()


def head_chunks(heads):
    groups = heads // GROUP
    if groups < 2:
        return ((0, heads),)
    first = max(1, int(groups * FIRST_PART)) * GROUP
    return ((0, first), (first, heads - first))


def exchange(x, axis, mask):
    count = lax.axis_size(axis)
    return lax.ppermute(x, axis, [(i, i ^ mask) for i in range(count)])


def cost(flops, nbytes):
    return pl.CostEstimate(flops=int(flops), bytes_accessed=int(nbytes), transcendentals=0)


def local(inputs, out_grad, w_query, w_key, w_value, w_output, saved_probs):
    seqs, length, width = inputs.shape
    heads = saved_probs.shape[1]
    size = width // heads
    cores, others = lax.axis_size("seqb"), lax.axis_size("seqa")
    rows = length // (cores * others)
    dims = (seqs, length, heads, size, cores, others, rows)
    radices = radices_of(others)
    lanes = seqs * size
    core, chip = lax.axis_index("seqb"), lax.axis_index("seqa")
    sc = jnp.stack([core, chip]).astype(jnp.int32)
    probs = jnp.swapaxes(saved_probs, 0, 1)
    params = pltpu.CompilerParams(vmem_limit_bytes=VMEM_LIMIT)
    proj = 2 * seqs * length * width * width
    mapf = 2 * heads * length * length * lanes
    smem = pl.BlockSpec(memory_space=pltpu.SMEM)
    vmem = pl.BlockSpec(memory_space=pltpu.VMEM)
    hbm = pl.BlockSpec(memory_space=pltpu.HBM)
    m_shape = lambda n: jax.ShapeDtypeStruct((others, n, rows, length), BF16)
    v_shape = lambda n: jax.ShapeDtypeStruct((n, length, lanes), BF16)
    like = lambda a: jax.ShapeDtypeStruct(a.shape, a.dtype)
    total_shape = jax.ShapeDtypeStruct(inputs.shape, F32)
    chunks = head_chunks(heads)

    def kernel(body, in_specs, outs, flops, nbytes, limit=VMEM_LIMIT, **more):
        specs = more.pop("out_specs", [vmem] * len(outs))
        return pl.pallas_call(
            body,
            in_specs=in_specs,
            out_specs=specs,
            out_shape=outs,
            compiler_params=pltpu.CompilerParams(vmem_limit_bytes=limit),
            cost_estimate=cost(flops, nbytes),
            **more,
        )

    a_alls, keeps, recvs = [], [], []
    for c, (first, n) in enumerate(chunks):
        share = n / heads
        if c == 0:
            in_hbm = [
                pltpu.with_memory_space_constraint(a, pltpu.HBM)
                for a in (inputs, w_value, out_grad, w_output)
            ]
            m_send, a_all, v_all, x_in, og_in, wo_in, wv_in = kernel(
                functools.partial(first_map_kernel, dims, radices),
                [smem, hbm, hbm, hbm, hbm],
                [m_shape(n), v_shape(n), v_shape(n), like(inputs), like(out_grad)]
                + [like(w_output), like(w_value)],
                share * (2 * proj + mapf / 2),
                8e6,
                scratch_shapes=[pltpu.SemaphoreType.DMA((4,))],
            )(sc, *in_hbm)
        else:
            m_send, a_all, v_all = kernel(
                functools.partial(map_send_kernel, dims, radices, first),
                [smem] + [vmem] * 4,
                [m_shape(n), v_shape(n), v_shape(n)],
                share * (2 * proj + mapf / 2),
                2e6,
            )(sc, x_in, wv_in, og_in, wo_in)
        recvs.append(exchange(m_send, "seqb", 1))
        keeps += kernel(
            functools.partial(map_keep_kernel, dims, radices),
            [smem, vmem, vmem],
            [m_shape(n)],
            share * mapf / 2,
            2e6,
        )(sc, a_all, v_all)
        a_alls.append(a_all)

    o_v, *p_rows = kernel(
        functools.partial(value_kernel, dims, chunks),
        [smem] + [vmem] * (len(chunks) + 2),
        [total_shape] + [jax.ShapeDtypeStruct((n, rows, length), F32) for _, n in chunks],
        proj + mapf,
        8e6,
        scratch_shapes=[pltpu.VMEM((seqs * length, width), BF16)],
    )(sc, *a_alls, wv_in, probs)
    q_all, k_all = kernel(
        functools.partial(query_key_kernel, dims),
        [vmem] * 3,
        [v_shape(heads), v_shape(heads)],
        2 * proj,
        6e6,
    )(x_in, w_query, w_key)

    small = lambda body, outs, count: kernel(body, [vmem] * count, outs, 1e6, 1e6, limit=6 << 20)
    logits = []
    for c, (first, n) in enumerate(chunks):
        shape = lambda k: radices[k:] + (n, rows, length)
        split = lambda k: [jax.ShapeDtypeStruct(shape(k + 1), F32)] + [
            jax.ShapeDtypeStruct(shape(k + 1), BF16)
        ] * (radices[k] - 1)
        keep, *sends = small(
            functools.partial(first_sum_kernel, radices[0]), split(0), 2
        )(keeps[c].reshape(shape(0)), recvs[c].reshape(shape(0)))
        shift = 0
        for k, r in enumerate(radices):
            terms = [exchange(x, "seqa", m << shift) for m, x in enumerate(sends, 1)]
            shift += r.bit_length() - 1
            if k + 1 < len(radices):
                keep, *sends = small(
                    functools.partial(sum_kernel, radices[k + 1], r), split(k + 1), r
                )(keep, *terms)
        logits += small(
            softmax_kernel, [jax.ShapeDtypeStruct((n, rows, length), BF16)], len(terms) + 2
        )(p_rows[c], keep, *terms)

    total = o_v
    for c, (first, n) in enumerate(chunks):
        last = c + 1 == len(chunks)
        parts = [logits[c]]
        shift = others.bit_length() - 1
        for k, r in list(enumerate(radices))[::-1]:
            block = jnp.stack(parts) if len(parts) > 1 else parts[0][None]
            if block.ndim > 4:
                block = block.reshape((-1,) + block.shape[2:])
            shift -= r.bit_length() - 1
            parts = [block] + [exchange(block, "seqa", m << shift) for m in range(1, r)]
        crossed = [exchange(p, "seqb", 1) for p in parts]
        total = kernel(
            functools.partial(post_kernel, dims, radices, chunks[c], last),
            [smem] + [vmem] * (2 * radices[0] + 5),
            total_shape,
            n / heads * (2 * proj + 2 * mapf),
            4e6,
            out_specs=hbm if last else vmem,
            scratch_shapes=[
                pltpu.VMEM((n, length, length), BF16),
                pltpu.VMEM((seqs * length, 2 * n * size), BF16),
            ]
            + (
                [pltpu.VMEM((seqs, length, width), F32), pltpu.SemaphoreType.DMA((seqs,))]
                if last
                else []
            ),
        )(sc, *parts, *crossed, q_all, k_all, w_query, w_key, total)
    return total


def solution(mesh):
    placed = (
        P(("grp", "seqa", "seqb"), None, None),
        P(("grp", "seqa", "seqb"), None, None),
        P(),
        P(),
        P(),
        P(),
        P("grp", None, None),
    )

    return jax.shard_map(
        local,
        mesh=mesh,
        in_specs=placed,
        out_specs=P(("grp", "seqa", "seqb"), None, None),
        check_vma=False,
    )
```

time: 57 us -> 59.1 us (1.037)
  starting transfers between devices: 12.2 us -> 27.4 us
  waiting for transfers between devices: 22.7 us -> 11 us
  Pallas kernels: 21.5 us -> 20.3 us
    ppermute x13 -> x26, starting transfers between devices: 12.2 us -> 27.4 us  [exchange(): return lax.ppermute(x, axis, [(i, i ^ mask) for i in range(count)])]
    ppermute x13 -> x26, waiting for transfers between devices: 22.7 us -> 11 us  [exchange(): return lax.ppermute(x, axis, [(i, i ^ mask) for i in range(count)])]
    pallas_call x8 -> x14, Pallas kernels: 21.5 us -> 20.3 us  [the longest x2 6.17 us: local(): kernel(functools.partial(post_kernel, dims, radices, chunks[c], last), [s...]
  transfers between devices with their start and end apart: 13 -> 26, of which waited for: 8 -> 5; matrix products, arithmetic and copies ran while one was open for 0% -> 0% of each run, Pallas kernels for 16% -> 21%
where the time goes in v2:
time: 59.1 us; the launch traced here: 59 us
  starting transfers between devices  27.4 us (46%)
  Pallas kernels  20.3 us (34%)
  waiting for transfers between devices  11 us (19%)
    ppermute x26, starting transfers between devices, exchange(): return lax.ppermute(x, axis, [(i, i ^ mask) for i in range(count)])  27.4 us
    ppermute x26, waiting for transfers between devices, exchange(): return lax.ppermute(x, axis, [(i, i ^ mask) for i in range(count)])  11 us
    pallas_call x2, Pallas kernels, local(): kernel(functools.partial(post_kernel, dims, radices, chunks[c], last), [s...  6.17 us
    pallas_call x1, Pallas kernels, local(): kernel(functools.partial(first_map_kernel, dims, radices), [smem, hbm, hb...  4.88 us
    pallas_call x1, Pallas kernels, local(): kernel(functools.partial(query_key_kernel, dims), [vmem] * 3, [v_shape(he...  2.7 us
    pallas_call x1, Pallas kernels, local(): kernel(functools.partial(value_kernel, dims, chunks), [smem] + [vmem] * (...  2.38 us
    pallas_call x2, Pallas kernels, local(): kernel(functools.partial(map_keep_kernel, dims, radices), [smem, vmem, vm...  1.86 us
    pallas_call x1, Pallas kernels, local(): kernel(functools.partial(map_send_kernel, dims, radices, first), [smem] +...  1.85 us
  transfers between devices with their start and end apart: 26, of which 5 were waited for; matrix products, arithmetic and copies ran while one was open for 0% of the time, Pallas kernels for 21%

profile of v2, /device:TPU:0, one launch (start us, length us, event | category | flops | bytes accessed | tf_op | source)
XLA Modules:
  0.0 59.0 jit_solution(16043464550454297105)
XLA Ops:
  0.0 0.1 pad_add_fusion.sc
  0.1 4.9 %shard_map.73 = (bf16[8,8,16,256]{3,2,1,0:T(8,128)(2,1)S(1)}, bf16[8,256,256]{2,1,0:T(8,128)(2,1)S(1)}, bf16[8,256,256]{2,1,0:T(8,128)(2,1)S(1)}, bf16[4,256,768...) custom-call(s32[2]{0:T(128)S(1)} %pad_add_fusion.sc, ...), custom_call_target="tpu_custom_call" | custom-call | flops 1744830464 | bytes 8000000 | tf_op jit(solution)/shard_map/pallas_call | solution.py:292
  5.0 0.6 collective-permute-start.13
  5.5 1.9 %shard_map.74 = (bf16[8,4,16,256]{3,2,1,0:T(8,128)(2,1)S(1)}, bf16[4,256,256]{2,1,0:T(8,128)(2,1)S(1)}, bf16[4,256,256]{2,1,0:T(8,128)(2,1)S(1)}) custom-call(s32[2]{0:T(128)S(1)} %pad_add_fusion.sc, bf16[4,256,768]{2,1,0:T(8,128)(2,1)S(1)} %get-tuple-element.33.x, bf16[768,768]{1,0:T(8,128)(2,1)S(1)} %get-tuple-element.34.wv.refs_2_, ...), custom_call_target="tpu_custom_call" | custom-call | flops 872415232 | bytes 2000000 | tf_op jit(solution)/shard_map/pallas_call | solution.py:302
  7.4 0.1 collective-permute-start
  7.5 1.0 %shard_map.81 = bf16[8,8,16,256]{3,2,1,0:T(8,128)(2,1)S(1)} custom-call(s32[2]{0:T(128)S(1)} %pad_add_fusion.sc, bf16[8,256,256]{2,1,0:T(8,128)(2,1)S(1)} %get-tuple-element.32.refs_0_.a_all, bf16[8,256,256]{2,1,0:T(8,128)(2,1)S(1)} %get-tuple-element.50.v_all), custom_call_target="tpu_custom_call" | custom-call | flops 134217728 | bytes 2000000 | tf_op jit(solution)/shard_map/pallas_call | solution.py:310
  8.5 0.0 copy-start.2
  8.5 0.1 shard_map.82
  8.6 3.1 %collective-permute-start.14 = (bf16[2,8,16,256]{3,2,1,0:T(8,128)(2,1)S(1)}, bf16[2,8,16,256]{3,2,1,0:T(8,128)(2,1)S(1)}, u32[]{:S(2)}, u32[]{:S(2)}) collective-permute-start(bf16[2,8,16,256]{3,2,1,0:T(8,128)(2,1)S(1)} %get-tuple-element.53), channel_id=1, source_target_pairs={{0,2},{2,0},{4,6},{6,4},{8,10},{10,8},{12,14},{14,12},{1,3},{3,1},... | collective-permute-start | bytes 393224 | tf_op jit(solution)/shard_map/ppermute | solution.py:241
  11.7 1.6 %collective-permute-start.15 = (bf16[2,8,16,256]{3,2,1,0:T(8,128)(2,1)S(1)}, bf16[2,8,16,256]{3,2,1,0:T(8,128)(2,1)S(1)}, u32[]{:S(2)}, u32[]{:S(2)}) collective-permute-start(bf16[2,8,16,256]{3,2,1,0:T(8,128)(2,1)S(1)} %get-tuple-element.54), channel_id=1, source_target_pairs={{0,4},{2,6},{4,0},{6,2},{8,12},{10,14},{12,8},{14,10},{1,5},{3,7},... | collective-permute-start | bytes 393224 | tf_op jit(solution)/shard_map/ppermute | solution.py:241
  13.3 0.8 %shard_map.76 = bf16[8,4,16,256]{3,2,1,0:T(8,128)(2,1)S(1)} custom-call(s32[2]{0:T(128)S(1)} %pad_add_fusion.sc, bf16[4,256,256]{2,1,0:T(8,128)(2,1)S(1)} %get-tuple-element.37.refs_1_.a_all, bf16[4,256,256]{2,1,0:T(8,128)(2,1)S(1)} %get-tuple-element.39.v_all), custom_call_target="tpu_custom_call" | custom-call | flops 67108864 | bytes 2000000 | tf_op jit(solution)/shard_map/pallas_call | solution.py:310
  14.1 0.1 shard_map.77
  14.2 2.0 %collective-permute-start.1 = (bf16[2,4,16,256]{3,2,1,0:T(8,128)(2,1)S(1)}, bf16[2,4,16,256]{3,2,1,0:T(8,128)(2,1)S(1)}, u32[]{:S(2)}, u32[]{:S(2)}) collective-permute-start(bf16[2,4,16,256]{3,2,1,0:T(8,128)(2,1)S(1)} %get-tuple-element.42), channel_id=1, source_target_pairs={{0,2},{2,0},{4,6},{6,4},{8,10},{10,8},{12,14},{14,12},{1,3},{3,1},... | collective-permute-start | bytes 196616 | tf_op jit(solution)/shard_map/ppermute | solution.py:241
  16.2 1.6 %collective-permute-start.2 = (bf16[2,4,16,256]{3,2,1,0:T(8,128)(2,1)S(1)}, bf16[2,4,16,256]{3,2,1,0:T(8,128)(2,1)S(1)}, u32[]{:S(2)}, u32[]{:S(2)}) collective-permute-start(bf16[2,4,16,256]{3,2,1,0:T(8,128)(2,1)S(1)} %get-tuple-element.43), channel_id=1, source_target_pairs={{0,4},{2,6},{4,0},{6,2},{8,12},{10,14},{12,8},{14,10},{1,5},{3,7},... | collective-permute-start | bytes 196616 | tf_op jit(solution)/shard_map/ppermute | solution.py:241
  17.8 0.4 collective-permute-start.3
  18.2 2.3 %collective-permute-done.16.refs_2_ = bf16[2,8,16,256]{3,2,1,0:T(8,128)(2,1)S(1)} collective-permute-done((bf16[2,8,16,256]{3,2,1,0:T(8,128)(2,1)S(1)}, bf16[2,8,16,256]{3,2,1,0:T(8,128)(2,1)S(1)}, u32[]{:S(2)}, u32[]{:S(2)}) %collective-permute-start.16) | collective-permute-done | bytes 131104 | tf_op jit(solution)/shard_map/ppermute | solution.py:241
  20.5 0.1 shard_map.83
  20.6 2.7 %collective-permute-start.17 = (bf16[8,16,256]{2,1,0:T(8,128)(2,1)S(1)}, bf16[8,16,256]{2,1,0:T(8,128)(2,1)S(1)}, u32[]{:S(2)}, u32[]{:S(2)}) collective-permute-start(bf16[8,16,256]{2,1,0:T(8,128)(2,1)S(1)} %get-tuple-element.57), channel_id=1, source_target_pairs={{0,8},{2,10},{4,12},{6,14},{8,0},{10,2},{12,4},{14,6},{1,9},{3,11}... | collective-permute-start | bytes 196616 | tf_op jit(solution)/shard_map/ppermute | solution.py:241
  23.3 2.4 %shard_map.75 = (f32[4,256,768]{2,1,0:T(8,128)S(1)}, f32[8,16,256]{2,1,0:T(8,128)S(1)}, f32[4,16,256]{2,1,0:T(8,128)S(1)}) custom-call(s32[2]{0:T(128)S(1)} %pad_add_fusion.sc, bf16[8,256,256]{2,1,0:T(8,128)(2,1)S(1)} %get-tuple-element.32.refs_0_.a_all, bf16[4,256,256]{2,1,0:T(8,128)(2,1)S(1)} %get-tuple-element.37.refs_1_.a_all, ...), custom_call_target="tpu_custom_call" | custom-call | flops 1610612736 | bytes 8000000 | tf_op jit(solution)/shard_map/pallas_call | solution.py:319
  25.7 0.1 collective-permute-done.17.refs_0_
  25.8 0.1 shard_map.84
  25.9 2.8 %collective-permute-start.18 = (bf16[1,8,16,256]{3,2,1,0:T(8,128)(2,1)S(1)}, bf16[1,8,16,256]{3,2,1,0:T(8,128)(2,1)S(1)}, u32[]{:S(2)}, u32[]{:S(2)}) collective-permute-start(bf16[1,8,16,256]{3,2,1,0:T(8,128)(2,1)S(1)} %bitcast.21), channel_id=1, source_target_pairs={{0,8},{2,10},{4,12},{6,14},{8,0},{10,2},{12,4},{14,6},{1,9},{3,11}... | collective-permute-start | bytes 196616 | tf_op jit(solution)/shard_map/ppermute | solution.py:241
  28.7 0.3 collective-permute-start.4
  29.0 4.8 %collective-permute-done.4.refs_0_ = bf16[4,16,256]{2,1,0:T(8,128)(2,1)S(1)} collective-permute-done((bf16[4,16,256]{2,1,0:T(8,128)(2,1)S(1)}, bf16[4,16,256]{2,1,0:T(8,128)(2,1)S(1)}, u32[]{:S(2)}, u32[]{:S(2)}) %collective-permute-start.4) | collective-permute-done | bytes 32800 | tf_op jit(solution)/shard_map/ppermute | solution.py:241
  33.8 0.1 shard_map.79
  33.9 0.6 collective-permute-start.5
  34.5 4.6 %collective-permute-start.21 = (bf16[2,8,16,256]{3,2,1,0:T(8,128)(2,1)S(1)}, bf16[2,8,16,256]{3,2,1,0:T(8,128)(2,1)S(1)}, u32[]{:S(2)}, u32[]{:S(2)}) collective-permute-start(bf16[2,8,16,256]{3,2,1,0:T(8,128)(2,1)S(1)} %maximum_bitcast_fusion.refs_0_), channel_id=1, source_target_pairs={{0,6},{2,4},{4,2},{6,0},{8,14},{10,12},{12,10},{14,8},{1,7},{3,5},... | collective-permute-start | bytes 393224 | tf_op jit(solution)/shard_map/ppermute | solution.py:241
  39.2 0.6 %collective-permute-start.19 = (bf16[2,8,16,256]{3,2,1,0:T(8,128)(2,1)S(1)}, bf16[2,8,16,256]{3,2,1,0:T(8,128)(2,1)S(1)}, u32[]{:S(2)}, u32[]{:S(2)}) collective-permute-start(bf16[2,8,16,256]{3,2,1,0:T(8,128)(2,1)S(1)} %maximum_bitcast_fusion.refs_0_), channel_id=1, source_target_pairs={{0,2},{2,0},{4,6},{6,4},{8,10},{10,8},{12,14},{14,12},{1,3},{3,1},... | collective-permute-start | bytes 393224 | tf_op jit(solution)/shard_map/ppermute | solution.py:241
  39.8 3.8 %collective-permute-start.8 = (bf16[2,4,16,256]{3,2,1,0:T(8,128)(2,1)S(1)}, bf16[2,4,16,256]{3,2,1,0:T(8,128)(2,1)S(1)}, u32[]{:S(2)}, u32[]{:S(2)}) collective-permute-start(bf16[2,4,16,256]{3,2,1,0:T(8,128)(2,1)S(1)} %maximum_bitcast_fusion.1.refs_0_), channel_id=1, source_target_pairs={{0,6},{2,4},{4,2},{6,0},{8,14},{10,12},{12,10},{14,8},{1,7},{3,5},... | collective-permute-start | bytes 196616 | tf_op jit(solution)/shard_map/ppermute | solution.py:241
  43.6 0.0 collective-permute-start.7
  43.6 2.2 %collective-permute-done.8.refs_3_ = bf16[2,4,16,256]{3,2,1,0:T(8,128)(2,1)S(1)} collective-permute-done((bf16[2,4,16,256]{3,2,1,0:T(8,128)(2,1)S(1)}, bf16[2,4,16,256]{3,2,1,0:T(8,128)(2,1)S(1)}, u32[]{:S(2)}, u32[]{:S(2)}) %collective-permute-start.8) | collective-permute-done | bytes 65568 | tf_op jit(solution)/shard_map/ppermute | solution.py:241
  45.9 0.6 collective-permute-start.6
  46.5 1.4 %collective-permute-done.7.refs_2_ = bf16[2,4,16,256]{3,2,1,0:T(8,128)(2,1)S(1)} collective-permute-done((bf16[2,4,16,256]{3,2,1,0:T(8,128)(2,1)S(1)}, bf16[2,4,16,256]{3,2,1,0:T(8,128)(2,1)S(1)}, u32[]{:S(2)}, u32[]{:S(2)}) %collective-permute-start.7) | collective-permute-done | bytes 65568 | tf_op jit(solution)/shard_map/ppermute | solution.py:241
  47.9 0.0 collective-permute-start.22
  47.9 0.5 collective-permute-start.25
  48.4 0.1 collective-permute-start.24
  48.5 0.0 collective-permute-done.19.refs_1_
  48.5 0.4 collective-permute-start.23
  48.9 2.7 %shard_map.80 = (bf16[12,256,256]{2,1,0:T(8,128)(2,1)S(1)}, bf16[12,256,256]{2,1,0:T(8,128)(2,1)S(1)}) custom-call(bf16[4,256,768]{2,1,0:T(8,128)(2,1)S(1)} %get-tuple-element.33.x, bf16[768,768]{1,0:T(8,128)(2,1)S(1)} %copy-done, bf16[768,768]{1,0:T(8,128)(2,1)S(1)} %copy-done.1), custom_call_target="tpu_custom_call" | custom-call | flops 2415919104 | bytes 6000000 | tf_op jit(solution)/shard_map/pallas_call | solution.py:327
  51.6 0.0 collective-permute-done.6.refs_1_
  51.6 0.1 collective-permute-start.9
  51.8 0.0 collective-permute-done.22.refs_4_
  51.8 0.4 collective-permute-start.12
  52.2 0.0 collective-permute-done.25.refs_7_
  52.2 0.1 collective-permute-start.11
  52.3 0.4 collective-permute-start.10
  52.7 3.0 %shard_map.85.refs_12_ = f32[4,256,768]{2,1,0:T(8,128)S(1)} custom-call(s32[2]{0:T(128)S(1)} %pad_add_fusion.sc, bf16[2,8,16,256]{3,2,1,0:T(8,128)(2,1)S(1)} %maximum_bitcast_fusion.refs_0_, bf16[2,8,16,256]{3,2,1,0:T(8,128)(2,1)S(1)} %collective-permute-done.19.refs_1_, bf16[2,8,16,256]{3,2,1,0:T(8,128)(2,1)S(1)} %collective-permute-done.20.refs_2_, ...), custom_call_target="tpu_custom_call" | custom-call | flops 2147483648 | bytes 4000000 | tf_op jit(solution)/shard_map/pallas_call | solution.py:369
  55.8 3.2 %shard_map.86 = f32[4,256,768]{2,1,0:T(8,128)} custom-call(s32[2]{0:T(128)S(1)} %pad_add_fusion.sc, bf16[2,4,16,256]{3,2,1,0:T(8,128)(2,1)S(1)} %maximum_bitcast_fusion.1.refs_0_, bf16[2,4,16,256]{3,2,1,0:T(8,128)(2,1)S(1)} %collective-permute-done.6.refs_1_, bf16[2,4,16,256]{3,2,1,0:T(8,128)(2,1)S(1)} %collective-permute-done.7.refs_2_, ...), custom_call_target="tpu_custom_call" | custom-call | flops 1073741824 | bytes 4000000 | tf_op jit(solution)/shard_map/pallas_call | solution.py:369
  (27 shorter events, 0.1 us)
Async XLA Ops:
  5.0 3.5 %collective-permute-start.13 = (bf16[8,8,16,256]{3,2,1,0:T(8,128)(2,1)S(1)}, bf16[8,8,16,256]{3,2,1,0:T(8,128)(2,1)S(1)}, u32[]{:S(2)}, u32[]{:S(2)}) collective-permute-start(bf16[8,8,16,256]{3,2,1,0:T(8,128)(2,1)S(1)} %get-tuple-element.51), channel_id=1, source_target_pairs={{0,1},{1,0},{2,3},{3,2},{4,5},{5,4},{6,7},{7,6},{8,9},{9,8},{10,11... | collective-permute-start | bytes 1572872 | tf_op jit(solution)/shard_map/ppermute | solution.py:241
  7.4 6.8 %collective-permute-start = (bf16[8,4,16,256]{3,2,1,0:T(8,128)(2,1)S(1)}, bf16[8,4,16,256]{3,2,1,0:T(8,128)(2,1)S(1)}, u32[]{:S(2)}, u32[]{:S(2)}) collective-permute-start(bf16[8,4,16,256]{3,2,1,0:T(8,128)(2,1)S(1)} %get-tuple-element.40), channel_id=1, source_target_pairs={{0,1},{1,0},{2,3},{3,2},{4,5},{5,4},{6,7},{7,6},{8,9},{9,8},{10,11... | collective-permute-start | bytes 786440 | tf_op jit(solution)/shard_map/ppermute | solution.py:241
  8.5 14.8 %copy-start.2 = (f32[256,12,256]{2,0,1:T(8,128)S(1)}, f32[256,12,256]{2,0,1:T(8,128)}, u32[]{:S(2)}) copy-start(f32[256,12,256]{2,0,1:T(8,128)} %param.13) | copy-start | bytes 9437188
  8.6 9.1 %collective-permute-start.14 = (bf16[2,8,16,256]{3,2,1,0:T(8,128)(2,1)S(1)}, bf16[2,8,16,256]{3,2,1,0:T(8,128)(2,1)S(1)}, u32[]{:S(2)}, u32[]{:S(2)}) collective-permute-start(bf16[2,8,16,256]{3,2,1,0:T(8,128)(2,1)S(1)} %get-tuple-element.53), channel_id=1, source_target_pairs={{0,2},{2,0},{4,6},{6,4},{8,10},{10,8},{12,14},{14,12},{1,3},{3,1},... | collective-permute-start | bytes 393224 | tf_op jit(solution)/shard_map/ppermute | solution.py:241
  11.7 6.5 %collective-permute-start.15 = (bf16[2,8,16,256]{3,2,1,0:T(8,128)(2,1)S(1)}, bf16[2,8,16,256]{3,2,1,0:T(8,128)(2,1)S(1)}, u32[]{:S(2)}, u32[]{:S(2)}) collective-permute-start(bf16[2,8,16,256]{3,2,1,0:T(8,128)(2,1)S(1)} %get-tuple-element.54), channel_id=1, source_target_pairs={{0,4},{2,6},{4,0},{6,2},{8,12},{10,14},{12,8},{14,10},{1,5},{3,7},... | collective-permute-start | bytes 393224 | tf_op jit(solution)/shard_map/ppermute | solution.py:241
  13.3 7.2 %collective-permute-start.16 = (bf16[2,8,16,256]{3,2,1,0:T(8,128)(2,1)S(1)}, bf16[2,8,16,256]{3,2,1,0:T(8,128)(2,1)S(1)}, u32[]{:S(2)}, u32[]{:S(2)}) collective-permute-start(bf16[2,8,16,256]{3,2,1,0:T(8,128)(2,1)S(1)} %get-tuple-element.55), channel_id=1, source_target_pairs={{0,6},{2,4},{4,2},{6,0},{8,14},{10,12},{12,10},{14,8},{1,7},{3,5},... | collective-permute-start | bytes 393224 | tf_op jit(solution)/shard_map/ppermute | solution.py:241
  14.2 14.5 %collective-permute-start.1 = (bf16[2,4,16,256]{3,2,1,0:T(8,128)(2,1)S(1)}, bf16[2,4,16,256]{3,2,1,0:T(8,128)(2,1)S(1)}, u32[]{:S(2)}, u32[]{:S(2)}) collective-permute-start(bf16[2,4,16,256]{3,2,1,0:T(8,128)(2,1)S(1)} %get-tuple-element.42), channel_id=1, source_target_pairs={{0,2},{2,0},{4,6},{6,4},{8,10},{10,8},{12,14},{14,12},{1,3},{3,1},... | collective-permute-start | bytes 196616 | tf_op jit(solution)/shard_map/ppermute | solution.py:241
  16.2 12.5 %collective-permute-start.2 = (bf16[2,4,16,256]{3,2,1,0:T(8,128)(2,1)S(1)}, bf16[2,4,16,256]{3,2,1,0:T(8,128)(2,1)S(1)}, u32[]{:S(2)}, u32[]{:S(2)}) collective-permute-start(bf16[2,4,16,256]{3,2,1,0:T(8,128)(2,1)S(1)} %get-tuple-element.43), channel_id=1, source_target_pairs={{0,4},{2,6},{4,0},{6,2},{8,12},{10,14},{12,8},{14,10},{1,5},{3,7},... | collective-permute-start | bytes 196616 | tf_op jit(solution)/shard_map/ppermute | solution.py:241
  17.8 10.9 %collective-permute-start.3 = (bf16[2,4,16,256]{3,2,1,0:T(8,128)(2,1)S(1)}, bf16[2,4,16,256]{3,2,1,0:T(8,128)(2,1)S(1)}, u32[]{:S(2)}, u32[]{:S(2)}) collective-permute-start(bf16[2,4,16,256]{3,2,1,0:T(8,128)(2,1)S(1)} %get-tuple-element.44), channel_id=1, source_target_pairs={{0,6},{2,4},{4,2},{6,0},{8,14},{10,12},{12,10},{14,8},{1,7},{3,5},... | collective-permute-start | bytes 196616 | tf_op jit(solution)/shard_map/ppermute | solution.py:241
  20.6 5.2 %collective-permute-start.17 = (bf16[8,16,256]{2,1,0:T(8,128)(2,1)S(1)}, bf16[8,16,256]{2,1,0:T(8,128)(2,1)S(1)}, u32[]{:S(2)}, u32[]{:S(2)}) collective-permute-start(bf16[8,16,256]{2,1,0:T(8,128)(2,1)S(1)} %get-tuple-element.57), channel_id=1, source_target_pairs={{0,8},{2,10},{4,12},{6,14},{8,0},{10,2},{12,4},{14,6},{1,9},{3,11}... | collective-permute-start | bytes 196616 | tf_op jit(solution)/shard_map/ppermute | solution.py:241
  23.3 25.6 %copy-start = (bf16[768,768]{1,0:T(8,128)(2,1)S(1)}, bf16[768,768]{1,0:T(8,128)(2,1)}, u32[]{:S(2)}) copy-start(bf16[768,768]{1,0:T(8,128)(2,1)} %refs_10_.3) | copy-start | bytes 3538948
  23.3 25.6 %copy-start.1 = (bf16[768,768]{1,0:T(8,128)(2,1)S(1)}, bf16[768,768]{1,0:T(8,128)(2,1)}, u32[]{:S(2)}) copy-start(bf16[768,768]{1,0:T(8,128)(2,1)} %refs_11_.3) | copy-start | bytes 3538948
  25.9 8.6 %collective-permute-start.18 = (bf16[1,8,16,256]{3,2,1,0:T(8,128)(2,1)S(1)}, bf16[1,8,16,256]{3,2,1,0:T(8,128)(2,1)S(1)}, u32[]{:S(2)}, u32[]{:S(2)}) collective-permute-start(bf16[1,8,16,256]{3,2,1,0:T(8,128)(2,1)S(1)} %bitcast.21), channel_id=1, source_target_pairs={{0,8},{2,10},{4,12},{6,14},{8,0},{10,2},{12,4},{14,6},{1,9},{3,11}... | collective-permute-start | bytes 196616 | tf_op jit(solution)/shard_map/ppermute | solution.py:241
  28.7 5.1 %collective-permute-start.4 = (bf16[4,16,256]{2,1,0:T(8,128)(2,1)S(1)}, bf16[4,16,256]{2,1,0:T(8,128)(2,1)S(1)}, u32[]{:S(2)}, u32[]{:S(2)}) collective-permute-start(bf16[4,16,256]{2,1,0:T(8,128)(2,1)S(1)} %get-tuple-element.46), channel_id=1, source_target_pairs={{0,8},{2,10},{4,12},{6,14},{8,0},{10,2},{12,4},{14,6},{1,9},{3,11}... | collective-permute-start | bytes 98312 | tf_op jit(solution)/shard_map/ppermute | solution.py:241
  33.9 5.9 %collective-permute-start.5 = (bf16[1,4,16,256]{3,2,1,0:T(8,128)(2,1)S(1)}, bf16[1,4,16,256]{3,2,1,0:T(8,128)(2,1)S(1)}, u32[]{:S(2)}, u32[]{:S(2)}) collective-permute-start(bf16[1,4,16,256]{3,2,1,0:T(8,128)(2,1)S(1)} %bitcast.23), channel_id=1, source_target_pairs={{0,8},{2,10},{4,12},{6,14},{8,0},{10,2},{12,4},{14,6},{1,9},{3,11}... | collective-permute-start | bytes 98312 | tf_op jit(solution)/shard_map/ppermute | solution.py:241
  34.5 13.4 %collective-permute-start.21 = (bf16[2,8,16,256]{3,2,1,0:T(8,128)(2,1)S(1)}, bf16[2,8,16,256]{3,2,1,0:T(8,128)(2,1)S(1)}, u32[]{:S(2)}, u32[]{:S(2)}) collective-permute-start(bf16[2,8,16,256]{3,2,1,0:T(8,128)(2,1)S(1)} %maximum_bitcast_fusion.refs_0_), channel_id=1, source_target_pairs={{0,6},{2,4},{4,2},{6,0},{8,14},{10,12},{12,10},{14,8},{1,7},{3,5},... | collective-permute-start | bytes 393224 | tf_op jit(solution)/shard_map/ppermute | solution.py:241
  39.2 9.3 %collective-permute-start.20 = (bf16[2,8,16,256]{3,2,1,0:T(8,128)(2,1)S(1)}, bf16[2,8,16,256]{3,2,1,0:T(8,128)(2,1)S(1)}, u32[]{:S(2)}, u32[]{:S(2)}) collective-permute-start(bf16[2,8,16,256]{3,2,1,0:T(8,128)(2,1)S(1)} %maximum_bitcast_fusion.refs_0_), channel_id=1, source_target_pairs={{0,4},{2,6},{4,0},{6,2},{8,12},{10,14},{12,8},{14,10},{1,5},{3,7},... | collective-permute-start | bytes 393224 | tf_op jit(solution)/shard_map/ppermute | solution.py:241
  39.2 9.3 %collective-permute-start.19 = (bf16[2,8,16,256]{3,2,1,0:T(8,128)(2,1)S(1)}, bf16[2,8,16,256]{3,2,1,0:T(8,128)(2,1)S(1)}, u32[]{:S(2)}, u32[]{:S(2)}) collective-permute-start(bf16[2,8,16,256]{3,2,1,0:T(8,128)(2,1)S(1)} %maximum_bitcast_fusion.refs_0_), channel_id=1, source_target_pairs={{0,2},{2,0},{4,6},{6,4},{8,10},{10,8},{12,14},{14,12},{1,3},{3,1},... | collective-permute-start | bytes 393224 | tf_op jit(solution)/shard_map/ppermute | solution.py:241
  39.8 6.1 %collective-permute-start.8 = (bf16[2,4,16,256]{3,2,1,0:T(8,128)(2,1)S(1)}, bf16[2,4,16,256]{3,2,1,0:T(8,128)(2,1)S(1)}, u32[]{:S(2)}, u32[]{:S(2)}) collective-permute-start(bf16[2,4,16,256]{3,2,1,0:T(8,128)(2,1)S(1)} %maximum_bitcast_fusion.1.refs_0_), channel_id=1, source_target_pairs={{0,6},{2,4},{4,2},{6,0},{8,14},{10,12},{12,10},{14,8},{1,7},{3,5},... | collective-permute-start | bytes 196616 | tf_op jit(solution)/shard_map/ppermute | solution.py:241
  43.6 4.3 %collective-permute-start.7 = (bf16[2,4,16,256]{3,2,1,0:T(8,128)(2,1)S(1)}, bf16[2,4,16,256]{3,2,1,0:T(8,128)(2,1)S(1)}, u32[]{:S(2)}, u32[]{:S(2)}) collective-permute-start(bf16[2,4,16,256]{3,2,1,0:T(8,128)(2,1)S(1)} %maximum_bitcast_fusion.1.refs_0_), channel_id=1, source_target_pairs={{0,4},{2,6},{4,0},{6,2},{8,12},{10,14},{12,8},{14,10},{1,5},{3,7},... | collective-permute-start | bytes 196616 | tf_op jit(solution)/shard_map/ppermute | solution.py:241
  45.9 5.8 %collective-permute-start.6 = (bf16[2,4,16,256]{3,2,1,0:T(8,128)(2,1)S(1)}, bf16[2,4,16,256]{3,2,1,0:T(8,128)(2,1)S(1)}, u32[]{:S(2)}, u32[]{:S(2)}) collective-permute-start(bf16[2,4,16,256]{3,2,1,0:T(8,128)(2,1)S(1)} %maximum_bitcast_fusion.1.refs_0_), channel_id=1, source_target_pairs={{0,2},{2,0},{4,6},{6,4},{8,10},{10,8},{12,14},{14,12},{1,3},{3,1},... | collective-permute-start | bytes 196616 | tf_op jit(solution)/shard_map/ppermute | solution.py:241
  47.9 3.9 %collective-permute-start.22 = (bf16[2,8,16,256]{3,2,1,0:T(8,128)(2,1)S(1)}, bf16[2,8,16,256]{3,2,1,0:T(8,128)(2,1)S(1)}, u32[]{:S(2)}, u32[]{:S(2)}) collective-permute-start(bf16[2,8,16,256]{3,2,1,0:T(8,128)(2,1)S(1)} %maximum_bitcast_fusion.refs_0_), channel_id=1, source_target_pairs={{0,1},{1,0},{2,3},{3,2},{4,5},{5,4},{6,7},{7,6},{8,9},{9,8},{10,11... | collective-permute-start | bytes 393224 | tf_op jit(solution)/shard_map/ppermute | solution.py:241
  47.9 4.3 %collective-permute-start.25 = (bf16[2,8,16,256]{3,2,1,0:T(8,128)(2,1)S(1)}, bf16[2,8,16,256]{3,2,1,0:T(8,128)(2,1)S(1)}, u32[]{:S(2)}, u32[]{:S(2)}) collective-permute-start(bf16[2,8,16,256]{3,2,1,0:T(8,128)(2,1)S(1)} %collective-permute-done.21.refs_3_), channel_id=1, source_target_pairs={{0,1},{1,0},{2,3},{3,2},{4,5},{5,4},{6,7},{7,6},{8,9},{9,8},{10,11... | collective-permute-start | bytes 393224 | tf_op jit(solution)/shard_map/ppermute | solution.py:241
  48.4 3.9 %collective-permute-start.24 = (bf16[2,8,16,256]{3,2,1,0:T(8,128)(2,1)S(1)}, bf16[2,8,16,256]{3,2,1,0:T(8,128)(2,1)S(1)}, u32[]{:S(2)}, u32[]{:S(2)}) collective-permute-start(bf16[2,8,16,256]{3,2,1,0:T(8,128)(2,1)S(1)} %collective-permute-done.20.refs_2_), channel_id=1, source_target_pairs={{0,1},{1,0},{2,3},{3,2},{4,5},{5,4},{6,7},{7,6},{8,9},{9,8},{10,11... | collective-permute-start | bytes 393224 | tf_op jit(solution)/shard_map/ppermute | solution.py:241
  48.5 4.3 %collective-permute-start.23 = (bf16[2,8,16,256]{3,2,1,0:T(8,128)(2,1)S(1)}, bf16[2,8,16,256]{3,2,1,0:T(8,128)(2,1)S(1)}, u32[]{:S(2)}, u32[]{:S(2)}) collective-permute-start(bf16[2,8,16,256]{3,2,1,0:T(8,128)(2,1)S(1)} %collective-permute-done.19.refs_1_), channel_id=1, source_target_pairs={{0,1},{1,0},{2,3},{3,2},{4,5},{5,4},{6,7},{7,6},{8,9},{9,8},{10,11... | collective-permute-start | bytes 393224 | tf_op jit(solution)/shard_map/ppermute | solution.py:241
  51.6 4.1 %collective-permute-start.9 = (bf16[2,4,16,256]{3,2,1,0:T(8,128)(2,1)S(1)}, bf16[2,4,16,256]{3,2,1,0:T(8,128)(2,1)S(1)}, u32[]{:S(2)}, u32[]{:S(2)}) collective-permute-start(bf16[2,4,16,256]{3,2,1,0:T(8,128)(2,1)S(1)} %maximum_bitcast_fusion.1.refs_0_), channel_id=1, source_target_pairs={{0,1},{1,0},{2,3},{3,2},{4,5},{5,4},{6,7},{7,6},{8,9},{9,8},{10,11... | collective-permute-start | bytes 196616 | tf_op jit(solution)/shard_map/ppermute | solution.py:241
  51.8 4.0 %collective-permute-start.12 = (bf16[2,4,16,256]{3,2,1,0:T(8,128)(2,1)S(1)}, bf16[2,4,16,256]{3,2,1,0:T(8,128)(2,1)S(1)}, u32[]{:S(2)}, u32[]{:S(2)}) collective-permute-start(bf16[2,4,16,256]{3,2,1,0:T(8,128)(2,1)S(1)} %collective-permute-done.8.refs_3_), channel_id=1, source_target_pairs={{0,1},{1,0},{2,3},{3,2},{4,5},{5,4},{6,7},{7,6},{8,9},{9,8},{10,11... | collective-permute-start | bytes 196616 | tf_op jit(solution)/shard_map/ppermute | solution.py:241
  52.2 3.6 %collective-permute-start.11 = (bf16[2,4,16,256]{3,2,1,0:T(8,128)(2,1)S(1)}, bf16[2,4,16,256]{3,2,1,0:T(8,128)(2,1)S(1)}, u32[]{:S(2)}, u32[]{:S(2)}) collective-permute-start(bf16[2,4,16,256]{3,2,1,0:T(8,128)(2,1)S(1)} %collective-permute-done.7.refs_2_), channel_id=1, source_target_pairs={{0,1},{1,0},{2,3},{3,2},{4,5},{5,4},{6,7},{7,6},{8,9},{9,8},{10,11... | collective-permute-start | bytes 196616 | tf_op jit(solution)/shard_map/ppermute | solution.py:241
  52.3 3.5 %collective-permute-start.10 = (bf16[2,4,16,256]{3,2,1,0:T(8,128)(2,1)S(1)}, bf16[2,4,16,256]{3,2,1,0:T(8,128)(2,1)S(1)}, u32[]{:S(2)}, u32[]{:S(2)}) collective-permute-start(bf16[2,4,16,256]{3,2,1,0:T(8,128)(2,1)S(1)} %collective-permute-done.6.refs_1_), channel_id=1, source_target_pairs={{0,1},{1,0},{2,3},{3,2},{4,5},{5,4},{6,7},{7,6},{8,9},{9,8},{10,11... | collective-permute-start | bytes 196616 | tf_op jit(solution)/shard_map/ppermute | solution.py:241

commit v3 on v2

--- a/solution.py
+++ b/solution.py
@@ -105,14 +105,32 @@
 def first_map_kernel(
     dims, radices, sc, x_hbm, wv_hbm, og_hbm, wo_hbm, m_out, a_out, v_out, x, og, wo, wv, sems
 ):
-    copies = fetch([(x_hbm, x), (wv_hbm, wv), (wo_hbm, wo), (og_hbm, og)], sems)
+    seqs, length, _, size = dims[:4]
+    used = pl.ds(0, v_out.shape[0] * size)
+    rest = pl.ds(v_out.shape[0] * size, wv.shape[1] - v_out.shape[0] * size)
+    pair = seqs // 2
+    halves = [pl.ds(0, pair), pl.ds(pair, seqs - pair)]
+    copies = fetch(
+        [(wv_hbm.at[:, used], wv.at[:, used])]
+        + [(x_hbm.at[part], x.at[part]) for part in halves]
+        + [(wo_hbm, wo), (og_hbm, og), (wv_hbm.at[:, rest], wv.at[:, rest])],
+        sems,
+    )
     copies[0].wait()
-    copies[1].wait()
-    value_rows(x, wv, v_out, 0, dims)
-    copies[2].wait()
+    for p, part in enumerate(halves):
+        copies[1 + p].wait()
+        count = seqs - pair if p else pair
+        flat = x[part].reshape(count * length, x.shape[-1])
+        at = p * pair * size
+        for a, b in groups_of(v_out.shape[0]):
+            v4 = dot_nn(flat, wv[:, a * size : b * size]).astype(BF16)
+            for h in range(b - a):
+                v_out[a + h, :, at : at + count * size] = gather_head(v4, count, h, size)
     copies[3].wait()
+    copies[4].wait()
     attn_rows(og, wo, a_out, 0, dims)
     map_rows(1 - sc[0], sc[1], a_out, v_out, m_out, dims, radices)
+    copies[5].wait()
 
 
 def map_send_kernel(dims, radices, first, sc, x, wv, og, wo, m_out, a_out, v_out):
@@ -190,7 +208,10 @@
     first_head, count = chunk
     first = radices[0]
     own, other = refs[:first], refs[first : 2 * first]
-    q_all, k_all, w_q, w_k, o_in, out, logit, grads = refs[2 * first : 2 * first + 8]
+    if last:
+        q_all, k_all, w_q, w_k, o_in, out, logit, grads, staged, sems = refs[2 * first :]
+    else:
+        q_all, k_all, grads, logit = refs[2 * first :]
     scale = (size * seqs * cores * others) ** -0.5
     half = length // cores
     inner = others // first
@@ -213,12 +234,9 @@
         for at, parts in ((0, qs), (width, ks)):
             for s, block in enumerate(spread_heads(parts, seqs, size)):
                 grads[s * length : (s + 1) * length, at + a * size : at + b * size] = block
-    lanes = slice(first_head * size, (first_head + count) * size)
-    weights = jnp.concatenate([w_q[:, lanes], w_k[:, lanes]], axis=1)
     if not last:
-        out[...] = o_in[...] + dot_nt(grads[...], weights).reshape(out.shape)
         return
-    staged, sems = refs[-2:]
+    weights = both_weights(w_q, w_k, first_head, count, size)
     copies = []
     for s in range(seqs):
         staged[s] = o_in[s] + dot_nt(grads[s * length : (s + 1) * length], weights)
@@ -226,6 +244,16 @@
         copies[-1].start()
     for c in copies:
         c.wait()
+
+
+def both_weights(w_q, w_k, first, count, size):
+    lanes = slice(first * size, (first + count) * size)
+    return jnp.concatenate([w_q[:, lanes], w_k[:, lanes]], axis=1)
+
+
+def back_kernel(dims, chunk, grads, w_q, w_k, o_in, out):
+    weights = both_weights(w_q, w_k, *chunk, dims[3])
+    out[...] = o_in[...] + dot_nt(grads[...], weights).reshape(out.shape)
 
 
 def head_chunks(heads):
@@ -296,7 +324,7 @@
                 + [like(w_output), like(w_value)],
                 share * (2 * proj + mapf / 2),
                 8e6,
-                scratch_shapes=[pltpu.SemaphoreType.DMA((4,))],
+                scratch_shapes=[pltpu.SemaphoreType.DMA((6,))],
             )(sc, *in_hbm)
         else:
             m_send, a_all, v_all = kernel(
@@ -366,23 +394,40 @@
             shift -= r.bit_length() - 1
             parts = [block] + [exchange(block, "seqa", m << shift) for m in range(1, r)]
         crossed = [exchange(p, "seqb", 1) for p in parts]
-        total = kernel(
-            functools.partial(post_kernel, dims, radices, chunks[c], last),
-            [smem] + [vmem] * (2 * radices[0] + 5),
-            total_shape,
-            n / heads * (2 * proj + 2 * mapf),
-            4e6,
-            out_specs=hbm if last else vmem,
-            scratch_shapes=[
-                pltpu.VMEM((n, length, length), BF16),
-                pltpu.VMEM((seqs * length, 2 * n * size), BF16),
-            ]
-            + (
-                [pltpu.VMEM((seqs, length, width), F32), pltpu.SemaphoreType.DMA((seqs,))]
-                if last
-                else []
-            ),
-        )(sc, *parts, *crossed, q_all, k_all, w_query, w_key, total)
+        grads_shape = (seqs * length, 2 * n * size)
+        logit_scratch = pltpu.VMEM((n, length, length), BF16)
+        flops = n / heads * 2 * mapf
+        if last:
+            total = kernel(
+                functools.partial(post_kernel, dims, radices, chunks[c], True),
+                [smem] + [vmem] * (2 * radices[0] + 5),
+                total_shape,
+                n / heads * 2 * proj + flops,
+                4e6,
+                out_specs=hbm,
+                scratch_shapes=[
+                    logit_scratch,
+                    pltpu.VMEM(grads_shape, BF16),
+                    pltpu.VMEM((seqs, length, width), F32),
+                    pltpu.SemaphoreType.DMA((seqs,)),
+                ],
+            )(sc, *parts, *crossed, q_all, k_all, w_query, w_key, total)
+        else:
+            (grads,) = kernel(
+                functools.partial(post_kernel, dims, radices, chunks[c], False),
+                [smem] + [vmem] * (2 * radices[0] + 2),
+                [jax.ShapeDtypeStruct(grads_shape, BF16)],
+                flops,
+                4e6,
+                scratch_shapes=[logit_scratch],
+            )(sc, *parts, *crossed, q_all, k_all)
+            (total,) = kernel(
+                functools.partial(back_kernel, dims, chunks[c]),
+                [vmem] * 4,
+                [total_shape],
+                n / heads * 2 * proj,
+                6e6,
+            )(grads, w_query, w_key, total)
     return total
 
 

time: 59.1 us -> 59.4 us (level)
    pallas_call x2 -> x3, Pallas kernels: 6.17 us -> 6.63 us  [the longest x1 3.15 us: local(): kernel(functools.partial(post_kernel, dims, radices, chunks[c], True), [s...]
where the time goes in v3:
time: 59.4 us; the launch traced here: 59.3 us
  starting transfers between devices  27.3 us (46%)
  Pallas kernels  20.6 us (35%)
  waiting for transfers between devices  11 us (19%)
    ppermute x26, starting transfers between devices, exchange(): return lax.ppermute(x, axis, [(i, i ^ mask) for i in range(count)])  27.3 us
    ppermute x26, waiting for transfers between devices, exchange(): return lax.ppermute(x, axis, [(i, i ^ mask) for i in range(count)])  11 us
    pallas_call x1, Pallas kernels, local(): kernel(functools.partial(first_map_kernel, dims, radices), [smem, hbm, hb...  4.77 us
    pallas_call x1, Pallas kernels, local(): kernel(functools.partial(post_kernel, dims, radices, chunks[c], True), [s...  3.15 us
    pallas_call x1, Pallas kernels, local(): kernel(functools.partial(query_key_kernel, dims), [vmem] * 3, [v_shape(he...  2.7 us
    pallas_call x1, Pallas kernels, local(): kernel(functools.partial(value_kernel, dims, chunks), [smem] + [vmem] * (...  2.39 us
    pallas_call x2, Pallas kernels, local(): kernel(functools.partial(map_keep_kernel, dims, radices), [smem, vmem, vm...  1.86 us
    pallas_call x1, Pallas kernels, local(): kernel(functools.partial(map_send_kernel, dims, radices, first), [smem] +...  1.85 us
  transfers between devices with their start and end apart: 26, of which 5 were waited for; matrix products, arithmetic and copies ran while one was open for 0% of the time, Pallas kernels for 21%

profile of v3, /device:TPU:0, one launch (start us, length us, event | category | flops | bytes accessed | tf_op | source)
XLA Modules:
  0.0 59.3 jit_solution(13881223062843782809)
XLA Ops:
  0.0 0.1 pad_add_fusion.sc
  0.1 4.8 %shard_map.73 = (bf16[8,8,16,256]{3,2,1,0:T(8,128)(2,1)S(1)}, bf16[8,256,256]{2,1,0:T(8,128)(2,1)S(1)}, bf16[8,256,256]{2,1,0:T(8,128)(2,1)S(1)}, bf16[4,256,768...) custom-call(s32[2]{0:T(128)S(1)} %pad_add_fusion.sc, ...), custom_call_target="tpu_custom_call" | custom-call | flops 1744830464 | bytes 8000000 | tf_op jit(solution)/shard_map/pallas_call | solution.py:320
  4.9 0.6 collective-permute-start.13
  5.4 1.9 %shard_map.74 = (bf16[8,4,16,256]{3,2,1,0:T(8,128)(2,1)S(1)}, bf16[4,256,256]{2,1,0:T(8,128)(2,1)S(1)}, bf16[4,256,256]{2,1,0:T(8,128)(2,1)S(1)}) custom-call(s32[2]{0:T(128)S(1)} %pad_add_fusion.sc, bf16[4,256,768]{2,1,0:T(8,128)(2,1)S(1)} %get-tuple-element.33.x, bf16[768,768]{1,0:T(8,128)(2,1)S(1)} %get-tuple-element.34.wv.refs_2_, ...), custom_call_target="tpu_custom_call" | custom-call | flops 872415232 | bytes 2000000 | tf_op jit(solution)/shard_map/pallas_call | solution.py:330
  7.3 0.1 collective-permute-start
  7.4 1.0 %shard_map.81 = bf16[8,8,16,256]{3,2,1,0:T(8,128)(2,1)S(1)} custom-call(s32[2]{0:T(128)S(1)} %pad_add_fusion.sc, bf16[8,256,256]{2,1,0:T(8,128)(2,1)S(1)} %get-tuple-element.32.refs_0_.a_all, bf16[8,256,256]{2,1,0:T(8,128)(2,1)S(1)} %get-tuple-element.50.v_all), custom_call_target="tpu_custom_call" | custom-call | flops 134217728 | bytes 2000000 | tf_op jit(solution)/shard_map/pallas_call | solution.py:338
  8.4 0.0 collective-permute-done.13
  8.4 0.0 copy-start.2
  8.4 0.1 shard_map.82
  8.5 3.1 %collective-permute-start.14 = (bf16[2,8,16,256]{3,2,1,0:T(8,128)(2,1)S(1)}, bf16[2,8,16,256]{3,2,1,0:T(8,128)(2,1)S(1)}, u32[]{:S(2)}, u32[]{:S(2)}) collective-permute-start(bf16[2,8,16,256]{3,2,1,0:T(8,128)(2,1)S(1)} %get-tuple-element.53), channel_id=1, source_target_pairs={{0,2},{2,0},{4,6},{6,4},{8,10},{10,8},{12,14},{14,12},{1,3},{3,1},... | collective-permute-start | bytes 393224 | tf_op jit(solution)/shard_map/ppermute | solution.py:269
  11.6 1.6 %collective-permute-start.15 = (bf16[2,8,16,256]{3,2,1,0:T(8,128)(2,1)S(1)}, bf16[2,8,16,256]{3,2,1,0:T(8,128)(2,1)S(1)}, u32[]{:S(2)}, u32[]{:S(2)}) collective-permute-start(bf16[2,8,16,256]{3,2,1,0:T(8,128)(2,1)S(1)} %get-tuple-element.54), channel_id=1, source_target_pairs={{0,4},{2,6},{4,0},{6,2},{8,12},{10,14},{12,8},{14,10},{1,5},{3,7},... | collective-permute-start | bytes 393224 | tf_op jit(solution)/shard_map/ppermute | solution.py:269
  13.2 0.0 collective-permute-start.16
  13.2 0.8 %shard_map.76 = bf16[8,4,16,256]{3,2,1,0:T(8,128)(2,1)S(1)} custom-call(s32[2]{0:T(128)S(1)} %pad_add_fusion.sc, bf16[4,256,256]{2,1,0:T(8,128)(2,1)S(1)} %get-tuple-element.37.refs_1_.a_all, bf16[4,256,256]{2,1,0:T(8,128)(2,1)S(1)} %get-tuple-element.39.v_all), custom_call_target="tpu_custom_call" | custom-call | flops 67108864 | bytes 2000000 | tf_op jit(solution)/shard_map/pallas_call | solution.py:338
  14.0 0.0 collective-permute-done
  14.0 0.1 shard_map.77
  14.1 2.0 %collective-permute-start.1 = (bf16[2,4,16,256]{3,2,1,0:T(8,128)(2,1)S(1)}, bf16[2,4,16,256]{3,2,1,0:T(8,128)(2,1)S(1)}, u32[]{:S(2)}, u32[]{:S(2)}) collective-permute-start(bf16[2,4,16,256]{3,2,1,0:T(8,128)(2,1)S(1)} %get-tuple-element.42), channel_id=1, source_target_pairs={{0,2},{2,0},{4,6},{6,4},{8,10},{10,8},{12,14},{14,12},{1,3},{3,1},... | collective-permute-start | bytes 196616 | tf_op jit(solution)/shard_map/ppermute | solution.py:269
  16.1 1.6 %collective-permute-start.2 = (bf16[2,4,16,256]{3,2,1,0:T(8,128)(2,1)S(1)}, bf16[2,4,16,256]{3,2,1,0:T(8,128)(2,1)S(1)}, u32[]{:S(2)}, u32[]{:S(2)}) collective-permute-start(bf16[2,4,16,256]{3,2,1,0:T(8,128)(2,1)S(1)} %get-tuple-element.43), channel_id=1, source_target_pairs={{0,4},{2,6},{4,0},{6,2},{8,12},{10,14},{12,8},{14,10},{1,5},{3,7},... | collective-permute-start | bytes 196616 | tf_op jit(solution)/shard_map/ppermute | solution.py:269
  17.6 0.0 collective-permute-done.14.refs_0_
  17.7 0.4 collective-permute-start.3
  18.1 0.0 collective-permute-done.15.refs_1_
  18.1 2.3 %collective-permute-done.16.refs_2_ = bf16[2,8,16,256]{3,2,1,0:T(8,128)(2,1)S(1)} collective-permute-done((bf16[2,8,16,256]{3,2,1,0:T(8,128)(2,1)S(1)}, bf16[2,8,16,256]{3,2,1,0:T(8,128)(2,1)S(1)}, u32[]{:S(2)}, u32[]{:S(2)}) %collective-permute-start.16) | collective-permute-done | bytes 131104 | tf_op jit(solution)/shard_map/ppermute | solution.py:269
  20.4 0.1 shard_map.83
  20.5 2.7 %collective-permute-start.17 = (bf16[8,16,256]{2,1,0:T(8,128)(2,1)S(1)}, bf16[8,16,256]{2,1,0:T(8,128)(2,1)S(1)}, u32[]{:S(2)}, u32[]{:S(2)}) collective-permute-start(bf16[8,16,256]{2,1,0:T(8,128)(2,1)S(1)} %get-tuple-element.57), channel_id=1, source_target_pairs={{0,8},{2,10},{4,12},{6,14},{8,0},{10,2},{12,4},{14,6},{1,9},{3,11}... | collective-permute-start | bytes 196616 | tf_op jit(solution)/shard_map/ppermute | solution.py:269
  23.2 2.4 %shard_map.75 = (f32[4,256,768]{2,1,0:T(8,128)S(1)}, f32[8,16,256]{2,1,0:T(8,128)S(1)}, f32[4,16,256]{2,1,0:T(8,128)S(1)}) custom-call(s32[2]{0:T(128)S(1)} %pad_add_fusion.sc, bf16[8,256,256]{2,1,0:T(8,128)(2,1)S(1)} %get-tuple-element.32.refs_0_.a_all, bf16[4,256,256]{2,1,0:T(8,128)(2,1)S(1)} %get-tuple-element.37.refs_1_.a_all, ...), custom_call_target="tpu_custom_call" | custom-call | flops 1610612736 | bytes 8000000 | tf_op jit(solution)/shard_map/pallas_call | solution.py:347
  25.6 0.1 collective-permute-done.17.refs_0_
  25.7 0.1 shard_map.84
  25.8 2.8 %collective-permute-start.18 = (bf16[1,8,16,256]{3,2,1,0:T(8,128)(2,1)S(1)}, bf16[1,8,16,256]{3,2,1,0:T(8,128)(2,1)S(1)}, u32[]{:S(2)}, u32[]{:S(2)}) collective-permute-start(bf16[1,8,16,256]{3,2,1,0:T(8,128)(2,1)S(1)} %bitcast.21), channel_id=1, source_target_pairs={{0,8},{2,10},{4,12},{6,14},{8,0},{10,2},{12,4},{14,6},{1,9},{3,11}... | collective-permute-start | bytes 196616 | tf_op jit(solution)/shard_map/ppermute | solution.py:269
  28.6 0.3 collective-permute-start.4
  28.9 4.8 %collective-permute-done.4.refs_0_ = bf16[4,16,256]{2,1,0:T(8,128)(2,1)S(1)} collective-permute-done((bf16[4,16,256]{2,1,0:T(8,128)(2,1)S(1)}, bf16[4,16,256]{2,1,0:T(8,128)(2,1)S(1)}, u32[]{:S(2)}, u32[]{:S(2)}) %collective-permute-start.4) | collective-permute-done | bytes 32800 | tf_op jit(solution)/shard_map/ppermute | solution.py:269
  33.8 0.1 shard_map.79
  33.8 0.5 collective-permute-start.5
  34.4 4.6 %collective-permute-start.21 = (bf16[2,8,16,256]{3,2,1,0:T(8,128)(2,1)S(1)}, bf16[2,8,16,256]{3,2,1,0:T(8,128)(2,1)S(1)}, u32[]{:S(2)}, u32[]{:S(2)}) collective-permute-start(bf16[2,8,16,256]{3,2,1,0:T(8,128)(2,1)S(1)} %maximum_bitcast_fusion.refs_0_), channel_id=1, source_target_pairs={{0,6},{2,4},{4,2},{6,0},{8,14},{10,12},{12,10},{14,8},{1,7},{3,5},... | collective-permute-start | bytes 393224 | tf_op jit(solution)/shard_map/ppermute | solution.py:269
  39.0 0.6 %collective-permute-start.19 = (bf16[2,8,16,256]{3,2,1,0:T(8,128)(2,1)S(1)}, bf16[2,8,16,256]{3,2,1,0:T(8,128)(2,1)S(1)}, u32[]{:S(2)}, u32[]{:S(2)}) collective-permute-start(bf16[2,8,16,256]{3,2,1,0:T(8,128)(2,1)S(1)} %maximum_bitcast_fusion.refs_0_), channel_id=1, source_target_pairs={{0,2},{2,0},{4,6},{6,4},{8,10},{10,8},{12,14},{14,12},{1,3},{3,1},... | collective-permute-start | bytes 393224 | tf_op jit(solution)/shard_map/ppermute | solution.py:269
  39.7 3.8 %collective-permute-start.8 = (bf16[2,4,16,256]{3,2,1,0:T(8,128)(2,1)S(1)}, bf16[2,4,16,256]{3,2,1,0:T(8,128)(2,1)S(1)}, u32[]{:S(2)}, u32[]{:S(2)}) collective-permute-start(bf16[2,4,16,256]{3,2,1,0:T(8,128)(2,1)S(1)} %maximum_bitcast_fusion.1.refs_0_), channel_id=1, source_target_pairs={{0,6},{2,4},{4,2},{6,0},{8,14},{10,12},{12,10},{14,8},{1,7},{3,5},... | collective-permute-start | bytes 196616 | tf_op jit(solution)/shard_map/ppermute | solution.py:269
  43.5 2.2 %collective-permute-done.8.refs_3_ = bf16[2,4,16,256]{3,2,1,0:T(8,128)(2,1)S(1)} collective-permute-done((bf16[2,4,16,256]{3,2,1,0:T(8,128)(2,1)S(1)}, bf16[2,4,16,256]{3,2,1,0:T(8,128)(2,1)S(1)}, u32[]{:S(2)}, u32[]{:S(2)}) %collective-permute-start.8) | collective-permute-done | bytes 65568 | tf_op jit(solution)/shard_map/ppermute | solution.py:269
  45.7 0.6 collective-permute-start.6
  46.3 1.4 %collective-permute-done.7.refs_2_ = bf16[2,4,16,256]{3,2,1,0:T(8,128)(2,1)S(1)} collective-permute-done((bf16[2,4,16,256]{3,2,1,0:T(8,128)(2,1)S(1)}, bf16[2,4,16,256]{3,2,1,0:T(8,128)(2,1)S(1)}, u32[]{:S(2)}, u32[]{:S(2)}) %collective-permute-start.7) | collective-permute-done | bytes 65568 | tf_op jit(solution)/shard_map/ppermute | solution.py:269
  47.8 0.5 collective-permute-start.25
  48.3 0.1 collective-permute-start.24
  48.3 0.4 collective-permute-start.23
  48.8 2.7 %shard_map.80 = (bf16[12,256,256]{2,1,0:T(8,128)(2,1)S(1)}, bf16[12,256,256]{2,1,0:T(8,128)(2,1)S(1)}) custom-call(bf16[4,256,768]{2,1,0:T(8,128)(2,1)S(1)} %get-tuple-element.33.x, bf16[768,768]{1,0:T(8,128)(2,1)S(1)} %copy-done, bf16[768,768]{1,0:T(8,128)(2,1)S(1)} %copy-done.1), custom_call_target="tpu_custom_call" | custom-call | flops 2415919104 | bytes 6000000 | tf_op jit(solution)/shard_map/pallas_call | solution.py:355
  51.5 0.1 collective-permute-start.9
  51.6 0.4 collective-permute-start.12
  52.1 0.1 collective-permute-start.11
  52.2 0.4 collective-permute-start.10
  52.6 1.6 %shard_map.85.grads = bf16[1024,1024]{1,0:T(8,128)(2,1)S(1)} custom-call(s32[2]{0:T(128)S(1)} %pad_add_fusion.sc, bf16[2,8,16,256]{3,2,1,0:T(8,128)(2,1)S(1)} %maximum_bitcast_fusion.refs_0_, bf16[2,8,16,256]{3,2,1,0:T(8,128)(2,1)S(1)} %collective-permute-done.19.refs_1_, bf16[2,8,16,256]{3,2,1,0:T(8,128)(2,1)S(1)} %collective-permute-done.20.refs_2_, ...), custom_call_target="tpu_custom_call" | custom-call | flops 536870912 | bytes 4000000 | tf_op jit(solution)/shard_map/pallas_call | solution.py:416
  54.2 1.8 %shard_map.86.refs_12_ = f32[4,256,768]{2,1,0:T(8,128)S(1)} custom-call(bf16[1024,1024]{1,0:T(8,128)(2,1)S(1)} %shard_map.85.grads, bf16[768,768]{1,0:T(8,128)(2,1)S(1)} %copy-done, bf16[768,768]{1,0:T(8,128)(2,1)S(1)} %copy-done.1, f32[4,256,768]{2,1,0:T(8,128)S(1)} %get-tuple-element.58.o_in), custom_call_target="tpu_custom_call" | custom-call | flops 1610612736 | bytes 6000000 | tf_op jit(solution)/shard_map/pallas_call | solution.py:424
  56.1 3.2 %shard_map.87 = f32[4,256,768]{2,1,0:T(8,128)} custom-call(s32[2]{0:T(128)S(1)} %pad_add_fusion.sc, bf16[2,4,16,256]{3,2,1,0:T(8,128)(2,1)S(1)} %maximum_bitcast_fusion.1.refs_0_, bf16[2,4,16,256]{3,2,1,0:T(8,128)(2,1)S(1)} %collective-permute-done.6.refs_1_, bf16[2,4,16,256]{3,2,1,0:T(8,128)(2,1)S(1)} %collective-permute-done.7.refs_2_, ...), custom_call_target="tpu_custom_call" | custom-call | flops 1073741824 | bytes 4000000 | tf_op jit(solution)/shard_map/pallas_call | solution.py:401
  (28 shorter events, 0.1 us)
Async XLA Ops:
  4.9 3.5 %collective-permute-start.13 = (bf16[8,8,16,256]{3,2,1,0:T(8,128)(2,1)S(1)}, bf16[8,8,16,256]{3,2,1,0:T(8,128)(2,1)S(1)}, u32[]{:S(2)}, u32[]{:S(2)}) collective-permute-start(bf16[8,8,16,256]{3,2,1,0:T(8,128)(2,1)S(1)} %get-tuple-element.51), channel_id=1, source_target_pairs={{0,1},{1,0},{2,3},{3,2},{4,5},{5,4},{6,7},{7,6},{8,9},{9,8},{10,11... | collective-permute-start | bytes 1572872 | tf_op jit(solution)/shard_map/ppermute | solution.py:269
  7.3 6.8 %collective-permute-start = (bf16[8,4,16,256]{3,2,1,0:T(8,128)(2,1)S(1)}, bf16[8,4,16,256]{3,2,1,0:T(8,128)(2,1)S(1)}, u32[]{:S(2)}, u32[]{:S(2)}) collective-permute-start(bf16[8,4,16,256]{3,2,1,0:T(8,128)(2,1)S(1)} %get-tuple-element.40), channel_id=1, source_target_pairs={{0,1},{1,0},{2,3},{3,2},{4,5},{5,4},{6,7},{7,6},{8,9},{9,8},{10,11... | collective-permute-start | bytes 786440 | tf_op jit(solution)/shard_map/ppermute | solution.py:269
  8.4 14.8 %copy-start.2 = (f32[256,12,256]{2,0,1:T(8,128)S(1)}, f32[256,12,256]{2,0,1:T(8,128)}, u32[]{:S(2)}) copy-start(f32[256,12,256]{2,0,1:T(8,128)} %param.13) | copy-start | bytes 9437188
  8.5 9.1 %collective-permute-start.14 = (bf16[2,8,16,256]{3,2,1,0:T(8,128)(2,1)S(1)}, bf16[2,8,16,256]{3,2,1,0:T(8,128)(2,1)S(1)}, u32[]{:S(2)}, u32[]{:S(2)}) collective-permute-start(bf16[2,8,16,256]{3,2,1,0:T(8,128)(2,1)S(1)} %get-tuple-element.53), channel_id=1, source_target_pairs={{0,2},{2,0},{4,6},{6,4},{8,10},{10,8},{12,14},{14,12},{1,3},{3,1},... | collective-permute-start | bytes 393224 | tf_op jit(solution)/shard_map/ppermute | solution.py:269
  11.6 6.5 %collective-permute-start.15 = (bf16[2,8,16,256]{3,2,1,0:T(8,128)(2,1)S(1)}, bf16[2,8,16,256]{3,2,1,0:T(8,128)(2,1)S(1)}, u32[]{:S(2)}, u32[]{:S(2)}) collective-permute-start(bf16[2,8,16,256]{3,2,1,0:T(8,128)(2,1)S(1)} %get-tuple-element.54), channel_id=1, source_target_pairs={{0,4},{2,6},{4,0},{6,2},{8,12},{10,14},{12,8},{14,10},{1,5},{3,7},... | collective-permute-start | bytes 393224 | tf_op jit(solution)/shard_map/ppermute | solution.py:269
  13.2 7.2 %collective-permute-start.16 = (bf16[2,8,16,256]{3,2,1,0:T(8,128)(2,1)S(1)}, bf16[2,8,16,256]{3,2,1,0:T(8,128)(2,1)S(1)}, u32[]{:S(2)}, u32[]{:S(2)}) collective-permute-start(bf16[2,8,16,256]{3,2,1,0:T(8,128)(2,1)S(1)} %get-tuple-element.55), channel_id=1, source_target_pairs={{0,6},{2,4},{4,2},{6,0},{8,14},{10,12},{12,10},{14,8},{1,7},{3,5},... | collective-permute-start | bytes 393224 | tf_op jit(solution)/shard_map/ppermute | solution.py:269
  14.1 14.5 %collective-permute-start.1 = (bf16[2,4,16,256]{3,2,1,0:T(8,128)(2,1)S(1)}, bf16[2,4,16,256]{3,2,1,0:T(8,128)(2,1)S(1)}, u32[]{:S(2)}, u32[]{:S(2)}) collective-permute-start(bf16[2,4,16,256]{3,2,1,0:T(8,128)(2,1)S(1)} %get-tuple-element.42), channel_id=1, source_target_pairs={{0,2},{2,0},{4,6},{6,4},{8,10},{10,8},{12,14},{14,12},{1,3},{3,1},... | collective-permute-start | bytes 196616 | tf_op jit(solution)/shard_map/ppermute | solution.py:269
  16.1 12.5 %collective-permute-start.2 = (bf16[2,4,16,256]{3,2,1,0:T(8,128)(2,1)S(1)}, bf16[2,4,16,256]{3,2,1,0:T(8,128)(2,1)S(1)}, u32[]{:S(2)}, u32[]{:S(2)}) collective-permute-start(bf16[2,4,16,256]{3,2,1,0:T(8,128)(2,1)S(1)} %get-tuple-element.43), channel_id=1, source_target_pairs={{0,4},{2,6},{4,0},{6,2},{8,12},{10,14},{12,8},{14,10},{1,5},{3,7},... | collective-permute-start | bytes 196616 | tf_op jit(solution)/shard_map/ppermute | solution.py:269
  17.7 10.9 %collective-permute-start.3 = (bf16[2,4,16,256]{3,2,1,0:T(8,128)(2,1)S(1)}, bf16[2,4,16,256]{3,2,1,0:T(8,128)(2,1)S(1)}, u32[]{:S(2)}, u32[]{:S(2)}) collective-permute-start(bf16[2,4,16,256]{3,2,1,0:T(8,128)(2,1)S(1)} %get-tuple-element.44), channel_id=1, source_target_pairs={{0,6},{2,4},{4,2},{6,0},{8,14},{10,12},{12,10},{14,8},{1,7},{3,5},... | collective-permute-start | bytes 196616 | tf_op jit(solution)/shard_map/ppermute | solution.py:269
  20.5 5.2 %collective-permute-start.17 = (bf16[8,16,256]{2,1,0:T(8,128)(2,1)S(1)}, bf16[8,16,256]{2,1,0:T(8,128)(2,1)S(1)}, u32[]{:S(2)}, u32[]{:S(2)}) collective-permute-start(bf16[8,16,256]{2,1,0:T(8,128)(2,1)S(1)} %get-tuple-element.57), channel_id=1, source_target_pairs={{0,8},{2,10},{4,12},{6,14},{8,0},{10,2},{12,4},{14,6},{1,9},{3,11}... | collective-permute-start | bytes 196616 | tf_op jit(solution)/shard_map/ppermute | solution.py:269
  23.2 25.6 %copy-start = (bf16[768,768]{1,0:T(8,128)(2,1)S(1)}, bf16[768,768]{1,0:T(8,128)(2,1)}, u32[]{:S(2)}) copy-start(bf16[768,768]{1,0:T(8,128)(2,1)} %refs_10_.1) | copy-start | bytes 3538948
  23.2 25.6 %copy-start.1 = (bf16[768,768]{1,0:T(8,128)(2,1)S(1)}, bf16[768,768]{1,0:T(8,128)(2,1)}, u32[]{:S(2)}) copy-start(bf16[768,768]{1,0:T(8,128)(2,1)} %refs_11_.1) | copy-start | bytes 3538948
  25.8 8.6 %collective-permute-start.18 = (bf16[1,8,16,256]{3,2,1,0:T(8,128)(2,1)S(1)}, bf16[1,8,16,256]{3,2,1,0:T(8,128)(2,1)S(1)}, u32[]{:S(2)}, u32[]{:S(2)}) collective-permute-start(bf16[1,8,16,256]{3,2,1,0:T(8,128)(2,1)S(1)} %bitcast.21), channel_id=1, source_target_pairs={{0,8},{2,10},{4,12},{6,14},{8,0},{10,2},{12,4},{14,6},{1,9},{3,11}... | collective-permute-start | bytes 196616 | tf_op jit(solution)/shard_map/ppermute | solution.py:269
  28.6 5.1 %collective-permute-start.4 = (bf16[4,16,256]{2,1,0:T(8,128)(2,1)S(1)}, bf16[4,16,256]{2,1,0:T(8,128)(2,1)S(1)}, u32[]{:S(2)}, u32[]{:S(2)}) collective-permute-start(bf16[4,16,256]{2,1,0:T(8,128)(2,1)S(1)} %get-tuple-element.46), channel_id=1, source_target_pairs={{0,8},{2,10},{4,12},{6,14},{8,0},{10,2},{12,4},{14,6},{1,9},{3,11}... | collective-permute-start | bytes 98312 | tf_op jit(solution)/shard_map/ppermute | solution.py:269
  33.8 5.8 %collective-permute-start.5 = (bf16[1,4,16,256]{3,2,1,0:T(8,128)(2,1)S(1)}, bf16[1,4,16,256]{3,2,1,0:T(8,128)(2,1)S(1)}, u32[]{:S(2)}, u32[]{:S(2)}) collective-permute-start(bf16[1,4,16,256]{3,2,1,0:T(8,128)(2,1)S(1)} %bitcast.23), channel_id=1, source_target_pairs={{0,8},{2,10},{4,12},{6,14},{8,0},{10,2},{12,4},{14,6},{1,9},{3,11}... | collective-permute-start | bytes 98312 | tf_op jit(solution)/shard_map/ppermute | solution.py:269
  34.4 13.4 %collective-permute-start.21 = (bf16[2,8,16,256]{3,2,1,0:T(8,128)(2,1)S(1)}, bf16[2,8,16,256]{3,2,1,0:T(8,128)(2,1)S(1)}, u32[]{:S(2)}, u32[]{:S(2)}) collective-permute-start(bf16[2,8,16,256]{3,2,1,0:T(8,128)(2,1)S(1)} %maximum_bitcast_fusion.refs_0_), channel_id=1, source_target_pairs={{0,6},{2,4},{4,2},{6,0},{8,14},{10,12},{12,10},{14,8},{1,7},{3,5},... | collective-permute-start | bytes 393224 | tf_op jit(solution)/shard_map/ppermute | solution.py:269
  39.0 9.2 %collective-permute-start.20 = (bf16[2,8,16,256]{3,2,1,0:T(8,128)(2,1)S(1)}, bf16[2,8,16,256]{3,2,1,0:T(8,128)(2,1)S(1)}, u32[]{:S(2)}, u32[]{:S(2)}) collective-permute-start(bf16[2,8,16,256]{3,2,1,0:T(8,128)(2,1)S(1)} %maximum_bitcast_fusion.refs_0_), channel_id=1, source_target_pairs={{0,4},{2,6},{4,0},{6,2},{8,12},{10,14},{12,8},{14,10},{1,5},{3,7},... | collective-permute-start | bytes 393224 | tf_op jit(solution)/shard_map/ppermute | solution.py:269
  39.0 9.3 %collective-permute-start.19 = (bf16[2,8,16,256]{3,2,1,0:T(8,128)(2,1)S(1)}, bf16[2,8,16,256]{3,2,1,0:T(8,128)(2,1)S(1)}, u32[]{:S(2)}, u32[]{:S(2)}) collective-permute-start(bf16[2,8,16,256]{3,2,1,0:T(8,128)(2,1)S(1)} %maximum_bitcast_fusion.refs_0_), channel_id=1, source_target_pairs={{0,2},{2,0},{4,6},{6,4},{8,10},{10,8},{12,14},{14,12},{1,3},{3,1},... | collective-permute-start | bytes 393224 | tf_op jit(solution)/shard_map/ppermute | solution.py:269
  39.7 6.0 %collective-permute-start.8 = (bf16[2,4,16,256]{3,2,1,0:T(8,128)(2,1)S(1)}, bf16[2,4,16,256]{3,2,1,0:T(8,128)(2,1)S(1)}, u32[]{:S(2)}, u32[]{:S(2)}) collective-permute-start(bf16[2,4,16,256]{3,2,1,0:T(8,128)(2,1)S(1)} %maximum_bitcast_fusion.1.refs_0_), channel_id=1, source_target_pairs={{0,6},{2,4},{4,2},{6,0},{8,14},{10,12},{12,10},{14,8},{1,7},{3,5},... | collective-permute-start | bytes 196616 | tf_op jit(solution)/shard_map/ppermute | solution.py:269
  43.5 4.3 %collective-permute-start.7 = (bf16[2,4,16,256]{3,2,1,0:T(8,128)(2,1)S(1)}, bf16[2,4,16,256]{3,2,1,0:T(8,128)(2,1)S(1)}, u32[]{:S(2)}, u32[]{:S(2)}) collective-permute-start(bf16[2,4,16,256]{3,2,1,0:T(8,128)(2,1)S(1)} %maximum_bitcast_fusion.1.refs_0_), channel_id=1, source_target_pairs={{0,4},{2,6},{4,0},{6,2},{8,12},{10,14},{12,8},{14,10},{1,5},{3,7},... | collective-permute-start | bytes 196616 | tf_op jit(solution)/shard_map/ppermute | solution.py:269
  45.7 5.8 %collective-permute-start.6 = (bf16[2,4,16,256]{3,2,1,0:T(8,128)(2,1)S(1)}, bf16[2,4,16,256]{3,2,1,0:T(8,128)(2,1)S(1)}, u32[]{:S(2)}, u32[]{:S(2)}) collective-permute-start(bf16[2,4,16,256]{3,2,1,0:T(8,128)(2,1)S(1)} %maximum_bitcast_fusion.1.refs_0_), channel_id=1, source_target_pairs={{0,2},{2,0},{4,6},{6,4},{8,10},{10,8},{12,14},{14,12},{1,3},{3,1},... | collective-permute-start | bytes 196616 | tf_op jit(solution)/shard_map/ppermute | solution.py:269
  47.8 3.9 %collective-permute-start.22 = (bf16[2,8,16,256]{3,2,1,0:T(8,128)(2,1)S(1)}, bf16[2,8,16,256]{3,2,1,0:T(8,128)(2,1)S(1)}, u32[]{:S(2)}, u32[]{:S(2)}) collective-permute-start(bf16[2,8,16,256]{3,2,1,0:T(8,128)(2,1)S(1)} %maximum_bitcast_fusion.refs_0_), channel_id=1, source_target_pairs={{0,1},{1,0},{2,3},{3,2},{4,5},{5,4},{6,7},{7,6},{8,9},{9,8},{10,11... | collective-permute-start | bytes 393224 | tf_op jit(solution)/shard_map/ppermute | solution.py:269
  47.8 4.3 %collective-permute-start.25 = (bf16[2,8,16,256]{3,2,1,0:T(8,128)(2,1)S(1)}, bf16[2,8,16,256]{3,2,1,0:T(8,128)(2,1)S(1)}, u32[]{:S(2)}, u32[]{:S(2)}) collective-permute-start(bf16[2,8,16,256]{3,2,1,0:T(8,128)(2,1)S(1)} %collective-permute-done.21.refs_3_), channel_id=1, source_target_pairs={{0,1},{1,0},{2,3},{3,2},{4,5},{5,4},{6,7},{7,6},{8,9},{9,8},{10,11... | collective-permute-start | bytes 393224 | tf_op jit(solution)/shard_map/ppermute | solution.py:269
  48.3 3.9 %collective-permute-start.24 = (bf16[2,8,16,256]{3,2,1,0:T(8,128)(2,1)S(1)}, bf16[2,8,16,256]{3,2,1,0:T(8,128)(2,1)S(1)}, u32[]{:S(2)}, u32[]{:S(2)}) collective-permute-start(bf16[2,8,16,256]{3,2,1,0:T(8,128)(2,1)S(1)} %collective-permute-done.20.refs_2_), channel_id=1, source_target_pairs={{0,1},{1,0},{2,3},{3,2},{4,5},{5,4},{6,7},{7,6},{8,9},{9,8},{10,11... | collective-permute-start | bytes 393224 | tf_op jit(solution)/shard_map/ppermute | solution.py:269
  48.3 4.3 %collective-permute-start.23 = (bf16[2,8,16,256]{3,2,1,0:T(8,128)(2,1)S(1)}, bf16[2,8,16,256]{3,2,1,0:T(8,128)(2,1)S(1)}, u32[]{:S(2)}, u32[]{:S(2)}) collective-permute-start(bf16[2,8,16,256]{3,2,1,0:T(8,128)(2,1)S(1)} %collective-permute-done.19.refs_1_), channel_id=1, source_target_pairs={{0,1},{1,0},{2,3},{3,2},{4,5},{5,4},{6,7},{7,6},{8,9},{9,8},{10,11... | collective-permute-start | bytes 393224 | tf_op jit(solution)/shard_map/ppermute | solution.py:269
  51.5 4.6 %collective-permute-start.9 = (bf16[2,4,16,256]{3,2,1,0:T(8,128)(2,1)S(1)}, bf16[2,4,16,256]{3,2,1,0:T(8,128)(2,1)S(1)}, u32[]{:S(2)}, u32[]{:S(2)}) collective-permute-start(bf16[2,4,16,256]{3,2,1,0:T(8,128)(2,1)S(1)} %maximum_bitcast_fusion.1.refs_0_), channel_id=1, source_target_pairs={{0,1},{1,0},{2,3},{3,2},{4,5},{5,4},{6,7},{7,6},{8,9},{9,8},{10,11... | collective-permute-start | bytes 196616 | tf_op jit(solution)/shard_map/ppermute | solution.py:269
  51.6 4.5 %collective-permute-start.12 = (bf16[2,4,16,256]{3,2,1,0:T(8,128)(2,1)S(1)}, bf16[2,4,16,256]{3,2,1,0:T(8,128)(2,1)S(1)}, u32[]{:S(2)}, u32[]{:S(2)}) collective-permute-start(bf16[2,4,16,256]{3,2,1,0:T(8,128)(2,1)S(1)} %collective-permute-done.8.refs_3_), channel_id=1, source_target_pairs={{0,1},{1,0},{2,3},{3,2},{4,5},{5,4},{6,7},{7,6},{8,9},{9,8},{10,11... | collective-permute-start | bytes 196616 | tf_op jit(solution)/shard_map/ppermute | solution.py:269
  52.1 4.0 %collective-permute-start.11 = (bf16[2,4,16,256]{3,2,1,0:T(8,128)(2,1)S(1)}, bf16[2,4,16,256]{3,2,1,0:T(8,128)(2,1)S(1)}, u32[]{:S(2)}, u32[]{:S(2)}) collective-permute-start(bf16[2,4,16,256]{3,2,1,0:T(8,128)(2,1)S(1)} %collective-permute-done.7.refs_2_), channel_id=1, source_target_pairs={{0,1},{1,0},{2,3},{3,2},{4,5},{5,4},{6,7},{7,6},{8,9},{9,8},{10,11... | collective-permute-start | bytes 196616 | tf_op jit(solution)/shard_map/ppermute | solution.py:269
  52.2 3.9 %collective-permute-start.10 = (bf16[2,4,16,256]{3,2,1,0:T(8,128)(2,1)S(1)}, bf16[2,4,16,256]{3,2,1,0:T(8,128)(2,1)S(1)}, u32[]{:S(2)}, u32[]{:S(2)}) collective-permute-start(bf16[2,4,16,256]{3,2,1,0:T(8,128)(2,1)S(1)} %collective-permute-done.6.refs_1_), channel_id=1, source_target_pairs={{0,1},{1,0},{2,3},{3,2},{4,5},{5,4},{6,7},{7,6},{8,9},{9,8},{10,11... | collective-permute-start | bytes 196616 | tf_op jit(solution)/shard_map/ppermute | solution.py:269

commit v4 on v3

--- a/solution.py
+++ b/solution.py
@@ -133,14 +133,18 @@
     copies[5].wait()
 
 
-def map_send_kernel(dims, radices, first, sc, x, wv, og, wo, m_out, a_out, v_out):
-    value_rows(x, wv, v_out, first, dims)
+def map_send_kernel(dims, radices, first, sc, v_all, og, wo, m_out, a_out):
     attn_rows(og, wo, a_out, first, dims)
-    map_rows(1 - sc[0], sc[1], a_out, v_out, m_out, dims, radices)
+    map_rows(1 - sc[0], sc[1], a_out, v_all, m_out, dims, radices)
 
 
 def map_keep_kernel(dims, radices, sc, a_all, v_all, m_out):
     map_rows(sc[0], sc[1], a_all, v_all, m_out, dims, radices)
+
+
+def first_keep_kernel(dims, radices, following, sc, a_all, v_all, x, wv, m_out, v_next):
+    map_rows(sc[0], sc[1], a_all, v_all, m_out, dims, radices)
+    value_rows(x, wv, v_next, following, dims)
 
 
 def value_kernel(dims, chunks, sc, *refs):
@@ -327,21 +331,33 @@
                 scratch_shapes=[pltpu.SemaphoreType.DMA((6,))],
             )(sc, *in_hbm)
         else:
-            m_send, a_all, v_all = kernel(
+            v_all = v_next
+            m_send, a_all = kernel(
                 functools.partial(map_send_kernel, dims, radices, first),
+                [smem] + [vmem] * 3,
+                [m_shape(n), v_shape(n)],
+                share * (proj + mapf / 2),
+                2e6,
+            )(sc, v_all, og_in, wo_in)
+        recvs.append(exchange(m_send, "seqb", 1))
+        if c == 0:
+            following, count = chunks[1]
+            m_keep, v_next = kernel(
+                functools.partial(first_keep_kernel, dims, radices, following),
                 [smem] + [vmem] * 4,
-                [m_shape(n), v_shape(n), v_shape(n)],
-                share * (2 * proj + mapf / 2),
+                [m_shape(n), v_shape(count)],
+                share * mapf / 2 + proj * count / heads,
+                3e6,
+            )(sc, a_all, v_all, x_in, wv_in)
+        else:
+            (m_keep,) = kernel(
+                functools.partial(map_keep_kernel, dims, radices),
+                [smem, vmem, vmem],
+                [m_shape(n)],
+                share * mapf / 2,
                 2e6,
-            )(sc, x_in, wv_in, og_in, wo_in)
-        recvs.append(exchange(m_send, "seqb", 1))
-        keeps += kernel(
-            functools.partial(map_keep_kernel, dims, radices),
-            [smem, vmem, vmem],
-            [m_shape(n)],
-            share * mapf / 2,
-            2e6,
-        )(sc, a_all, v_all)
+            )(sc, a_all, v_all)
+        keeps.append(m_keep)
         a_alls.append(a_all)
 
     o_v, *p_rows = kernel(

time: 59.4 us -> 59.7 us (level)
    pallas_call x0 -> x1, Pallas kernels: none -> 1.51 us  [local(): kernel(functools.partial(first_keep_kernel, dims, radices, following), [s...]
    pallas_call x2 -> x1, Pallas kernels: 1.86 us -> 0.84 us  [local(): kernel(functools.partial(map_keep_kernel, dims, radices), [smem, vmem, vm...]
  transfers between devices with their start and end apart: 26 -> 26, of which waited for: 5 -> 5; matrix products, arithmetic and copies ran while one was open for 0% -> 0% of each run, Pallas kernels for 21% -> 22%
where the time goes in v4:
time: 59.7 us; the launch traced here: 59.6 us
  starting transfers between devices  27.2 us (46%)
  Pallas kernels  21 us (35%)
  waiting for transfers between devices  11 us (18%)
    ppermute x26, starting transfers between devices, exchange(): return lax.ppermute(x, axis, [(i, i ^ mask) for i in range(count)])  27.2 us
    ppermute x26, waiting for transfers between devices, exchange(): return lax.ppermute(x, axis, [(i, i ^ mask) for i in range(count)])  11 us
    pallas_call x1, Pallas kernels, local(): kernel(functools.partial(first_map_kernel, dims, radices), [smem, hbm, hb...  4.77 us
    pallas_call x1, Pallas kernels, local(): kernel(functools.partial(post_kernel, dims, radices, chunks[c], True), [s...  3.15 us
    pallas_call x1, Pallas kernels, local(): kernel(functools.partial(query_key_kernel, dims), [vmem] * 3, [v_shape(he...  2.7 us
    pallas_call x1, Pallas kernels, local(): kernel(functools.partial(value_kernel, dims, chunks), [smem] + [vmem] * (...  2.38 us
    pallas_call x1, Pallas kernels, local(): kernel(functools.partial(back_kernel, dims, chunks[c]), [vmem] * 4, [tota...  1.84 us
    pallas_call x1, Pallas kernels, local(): kernel(functools.partial(map_send_kernel, dims, radices, first), [smem] +...  1.7 us
  transfers between devices with their start and end apart: 26, of which 5 were waited for; matrix products, arithmetic and copies ran while one was open for 0% of the time, Pallas kernels for 22%

profile of v4, /device:TPU:0, one launch (start us, length us, event | category | flops | bytes accessed | tf_op | source)
XLA Modules:
  0.0 59.6 jit_solution(10802913092136900029)
XLA Ops:
  0.0 0.1 pad_add_fusion.sc
  0.1 4.8 %shard_map.73 = (bf16[8,8,16,256]{3,2,1,0:T(8,128)(2,1)S(1)}, bf16[8,256,256]{2,1,0:T(8,128)(2,1)S(1)}, bf16[8,256,256]{2,1,0:T(8,128)(2,1)S(1)}, bf16[4,256,768...) custom-call(s32[2]{0:T(128)S(1)} %pad_add_fusion.sc, ...), custom_call_target="tpu_custom_call" | custom-call | flops 1744830464 | bytes 8000000 | tf_op jit(solution)/shard_map/pallas_call | solution.py:324
  4.9 0.6 collective-permute-start.13
  5.4 1.5 %shard_map.74 = (bf16[8,8,16,256]{3,2,1,0:T(8,128)(2,1)S(1)}, bf16[4,256,256]{2,1,0:T(8,128)(2,1)S(1)}) custom-call(s32[2]{0:T(128)S(1)} %pad_add_fusion.sc, bf16[8,256,256]{2,1,0:T(8,128)(2,1)S(1)} %get-tuple-element.33.a_all.refs_0_, bf16[8,256,256]{2,1,0:T(8,128)(2,1)S(1)} %get-tuple-element.34.v_all, bf16[4,256,768]{2,1,0:T(8,128)(2,1)S(1)} %get-tuple-element.35.x, ...), custom_call_target="tpu_custom_call" | custom-call | flops 536870912 | bytes 3000000 | tf_op jit(solution)/shard_map/pallas_call | solution.py:345
  6.9 1.7 %shard_map.75 = (bf16[8,4,16,256]{3,2,1,0:T(8,128)(2,1)S(1)}, bf16[4,256,256]{2,1,0:T(8,128)(2,1)S(1)}) custom-call(s32[2]{0:T(128)S(1)} %pad_add_fusion.sc, bf16[4,256,256]{2,1,0:T(8,128)(2,1)S(1)} %get-tuple-element.37.v_all, bf16[4,256,768]{2,1,0:T(8,128)(2,1)S(1)} %get-tuple-element.38.og, bf16[768,768]{1,0:T(8,128)(2,1)S(1)} %get-tuple-element.39.wo), custom_call_target="tpu_custom_call" | custom-call | flops 469762048 | bytes 2000000 | tf_op jit(solution)/shard_map/pallas_call | solution.py:335
  8.6 0.1 collective-permute-start
  8.7 0.0 collective-permute-done.13
  8.7 0.0 copy-start.2
  8.7 0.1 shard_map.82
  8.9 3.1 %collective-permute-start.14 = (bf16[2,8,16,256]{3,2,1,0:T(8,128)(2,1)S(1)}, bf16[2,8,16,256]{3,2,1,0:T(8,128)(2,1)S(1)}, u32[]{:S(2)}, u32[]{:S(2)}) collective-permute-start(bf16[2,8,16,256]{3,2,1,0:T(8,128)(2,1)S(1)} %get-tuple-element.55), channel_id=1, source_target_pairs={{0,2},{2,0},{4,6},{6,4},{8,10},{10,8},{12,14},{14,12},{1,3},{3,1},... | collective-permute-start | bytes 393224 | tf_op jit(solution)/shard_map/ppermute | solution.py:273
  11.9 1.6 %collective-permute-start.15 = (bf16[2,8,16,256]{3,2,1,0:T(8,128)(2,1)S(1)}, bf16[2,8,16,256]{3,2,1,0:T(8,128)(2,1)S(1)}, u32[]{:S(2)}, u32[]{:S(2)}) collective-permute-start(bf16[2,8,16,256]{3,2,1,0:T(8,128)(2,1)S(1)} %get-tuple-element.56), channel_id=1, source_target_pairs={{0,4},{2,6},{4,0},{6,2},{8,12},{10,14},{12,8},{14,10},{1,5},{3,7},... | collective-permute-start | bytes 393224 | tf_op jit(solution)/shard_map/ppermute | solution.py:273
  13.5 0.8 %shard_map.77 = bf16[8,4,16,256]{3,2,1,0:T(8,128)(2,1)S(1)} custom-call(s32[2]{0:T(128)S(1)} %pad_add_fusion.sc, bf16[4,256,256]{2,1,0:T(8,128)(2,1)S(1)} %get-tuple-element.40.refs_1_.a_all, bf16[4,256,256]{2,1,0:T(8,128)(2,1)S(1)} %get-tuple-element.37.v_all), custom_call_target="tpu_custom_call" | custom-call | flops 67108864 | bytes 2000000 | tf_op jit(solution)/shard_map/pallas_call | solution.py:353
  14.3 0.0 collective-permute-done
  14.4 0.1 shard_map.78
  14.4 2.0 %collective-permute-start.1 = (bf16[2,4,16,256]{3,2,1,0:T(8,128)(2,1)S(1)}, bf16[2,4,16,256]{3,2,1,0:T(8,128)(2,1)S(1)}, u32[]{:S(2)}, u32[]{:S(2)}) collective-permute-start(bf16[2,4,16,256]{3,2,1,0:T(8,128)(2,1)S(1)} %get-tuple-element.44), channel_id=1, source_target_pairs={{0,2},{2,0},{4,6},{6,4},{8,10},{10,8},{12,14},{14,12},{1,3},{3,1},... | collective-permute-start | bytes 196616 | tf_op jit(solution)/shard_map/ppermute | solution.py:273
  16.4 1.6 %collective-permute-start.2 = (bf16[2,4,16,256]{3,2,1,0:T(8,128)(2,1)S(1)}, bf16[2,4,16,256]{3,2,1,0:T(8,128)(2,1)S(1)}, u32[]{:S(2)}, u32[]{:S(2)}) collective-permute-start(bf16[2,4,16,256]{3,2,1,0:T(8,128)(2,1)S(1)} %get-tuple-element.45), channel_id=1, source_target_pairs={{0,4},{2,6},{4,0},{6,2},{8,12},{10,14},{12,8},{14,10},{1,5},{3,7},... | collective-permute-start | bytes 196616 | tf_op jit(solution)/shard_map/ppermute | solution.py:273
  18.0 0.0 collective-permute-done.14.refs_0_
  18.0 0.4 collective-permute-start.3
  18.4 2.4 %collective-permute-done.16.refs_2_ = bf16[2,8,16,256]{3,2,1,0:T(8,128)(2,1)S(1)} collective-permute-done((bf16[2,8,16,256]{3,2,1,0:T(8,128)(2,1)S(1)}, bf16[2,8,16,256]{3,2,1,0:T(8,128)(2,1)S(1)}, u32[]{:S(2)}, u32[]{:S(2)}) %collective-permute-start.16) | collective-permute-done | bytes 131104 | tf_op jit(solution)/shard_map/ppermute | solution.py:273
  20.7 0.1 shard_map.83
  20.8 2.7 %collective-permute-start.17 = (bf16[8,16,256]{2,1,0:T(8,128)(2,1)S(1)}, bf16[8,16,256]{2,1,0:T(8,128)(2,1)S(1)}, u32[]{:S(2)}, u32[]{:S(2)}) collective-permute-start(bf16[8,16,256]{2,1,0:T(8,128)(2,1)S(1)} %get-tuple-element.59), channel_id=1, source_target_pairs={{0,8},{2,10},{4,12},{6,14},{8,0},{10,2},{12,4},{14,6},{1,9},{3,11}... | collective-permute-start | bytes 196616 | tf_op jit(solution)/shard_map/ppermute | solution.py:273
  23.5 2.4 %shard_map.76 = (f32[4,256,768]{2,1,0:T(8,128)S(1)}, f32[8,16,256]{2,1,0:T(8,128)S(1)}, f32[4,16,256]{2,1,0:T(8,128)S(1)}) custom-call(s32[2]{0:T(128)S(1)} %pad_add_fusion.sc, bf16[8,256,256]{2,1,0:T(8,128)(2,1)S(1)} %get-tuple-element.33.a_all.refs_0_, bf16[4,256,256]{2,1,0:T(8,128)(2,1)S(1)} %get-tuple-element.40.refs_1_.a_all, ...), custom_call_target="tpu_custom_call" | custom-call | flops 1610612736 | bytes 8000000 | tf_op jit(solution)/shard_map/pallas_call | solution.py:363
  25.9 0.1 collective-permute-done.17.refs_0_
  26.0 0.1 shard_map.84
  26.1 2.7 %collective-permute-start.18 = (bf16[1,8,16,256]{3,2,1,0:T(8,128)(2,1)S(1)}, bf16[1,8,16,256]{3,2,1,0:T(8,128)(2,1)S(1)}, u32[]{:S(2)}, u32[]{:S(2)}) collective-permute-start(bf16[1,8,16,256]{3,2,1,0:T(8,128)(2,1)S(1)} %bitcast.21), channel_id=1, source_target_pairs={{0,8},{2,10},{4,12},{6,14},{8,0},{10,2},{12,4},{14,6},{1,9},{3,11}... | collective-permute-start | bytes 196616 | tf_op jit(solution)/shard_map/ppermute | solution.py:273
  28.9 0.0 collective-permute-done.1.refs_0_
  28.9 0.0 collective-permute-done.2.refs_1_
  28.9 0.3 collective-permute-start.4
  29.2 4.9 %collective-permute-done.4.refs_0_ = bf16[4,16,256]{2,1,0:T(8,128)(2,1)S(1)} collective-permute-done((bf16[4,16,256]{2,1,0:T(8,128)(2,1)S(1)}, bf16[4,16,256]{2,1,0:T(8,128)(2,1)S(1)}, u32[]{:S(2)}, u32[]{:S(2)}) %collective-permute-start.4) | collective-permute-done | bytes 32800 | tf_op jit(solution)/shard_map/ppermute | solution.py:273
  34.1 0.1 shard_map.80
  34.2 0.4 collective-permute-start.5
  34.7 4.7 %collective-permute-start.21 = (bf16[2,8,16,256]{3,2,1,0:T(8,128)(2,1)S(1)}, bf16[2,8,16,256]{3,2,1,0:T(8,128)(2,1)S(1)}, u32[]{:S(2)}, u32[]{:S(2)}) collective-permute-start(bf16[2,8,16,256]{3,2,1,0:T(8,128)(2,1)S(1)} %maximum_bitcast_fusion.refs_0_), channel_id=1, source_target_pairs={{0,6},{2,4},{4,2},{6,0},{8,14},{10,12},{12,10},{14,8},{1,7},{3,5},... | collective-permute-start | bytes 393224 | tf_op jit(solution)/shard_map/ppermute | solution.py:273
  39.4 0.6 %collective-permute-start.19 = (bf16[2,8,16,256]{3,2,1,0:T(8,128)(2,1)S(1)}, bf16[2,8,16,256]{3,2,1,0:T(8,128)(2,1)S(1)}, u32[]{:S(2)}, u32[]{:S(2)}) collective-permute-start(bf16[2,8,16,256]{3,2,1,0:T(8,128)(2,1)S(1)} %maximum_bitcast_fusion.refs_0_), channel_id=1, source_target_pairs={{0,2},{2,0},{4,6},{6,4},{8,10},{10,8},{12,14},{14,12},{1,3},{3,1},... | collective-permute-start | bytes 393224 | tf_op jit(solution)/shard_map/ppermute | solution.py:273
  40.0 3.8 %collective-permute-start.8 = (bf16[2,4,16,256]{3,2,1,0:T(8,128)(2,1)S(1)}, bf16[2,4,16,256]{3,2,1,0:T(8,128)(2,1)S(1)}, u32[]{:S(2)}, u32[]{:S(2)}) collective-permute-start(bf16[2,4,16,256]{3,2,1,0:T(8,128)(2,1)S(1)} %maximum_bitcast_fusion.1.refs_0_), channel_id=1, source_target_pairs={{0,6},{2,4},{4,2},{6,0},{8,14},{10,12},{12,10},{14,8},{1,7},{3,5},... | collective-permute-start | bytes 196616 | tf_op jit(solution)/shard_map/ppermute | solution.py:273
  43.8 2.2 %collective-permute-done.8.refs_3_ = bf16[2,4,16,256]{3,2,1,0:T(8,128)(2,1)S(1)} collective-permute-done((bf16[2,4,16,256]{3,2,1,0:T(8,128)(2,1)S(1)}, bf16[2,4,16,256]{3,2,1,0:T(8,128)(2,1)S(1)}, u32[]{:S(2)}, u32[]{:S(2)}) %collective-permute-start.8) | collective-permute-done | bytes 65568 | tf_op jit(solution)/shard_map/ppermute | solution.py:273
  46.0 0.6 %collective-permute-start.6 = (bf16[2,4,16,256]{3,2,1,0:T(8,128)(2,1)S(1)}, bf16[2,4,16,256]{3,2,1,0:T(8,128)(2,1)S(1)}, u32[]{:S(2)}, u32[]{:S(2)}) collective-permute-start(bf16[2,4,16,256]{3,2,1,0:T(8,128)(2,1)S(1)} %maximum_bitcast_fusion.1.refs_0_), channel_id=1, source_target_pairs={{0,2},{2,0},{4,6},{6,4},{8,10},{10,8},{12,14},{14,12},{1,3},{3,1},... | collective-permute-start | bytes 196616 | tf_op jit(solution)/shard_map/ppermute | solution.py:273
  46.6 1.4 %collective-permute-done.7.refs_2_ = bf16[2,4,16,256]{3,2,1,0:T(8,128)(2,1)S(1)} collective-permute-done((bf16[2,4,16,256]{3,2,1,0:T(8,128)(2,1)S(1)}, bf16[2,4,16,256]{3,2,1,0:T(8,128)(2,1)S(1)}, u32[]{:S(2)}, u32[]{:S(2)}) %collective-permute-start.7) | collective-permute-done | bytes 65568 | tf_op jit(solution)/shard_map/ppermute | solution.py:273
  48.1 0.5 collective-permute-start.25
  48.6 0.1 collective-permute-start.24
  48.6 0.4 collective-permute-start.23
  49.1 2.7 %shard_map.81 = (bf16[12,256,256]{2,1,0:T(8,128)(2,1)S(1)}, bf16[12,256,256]{2,1,0:T(8,128)(2,1)S(1)}) custom-call(bf16[4,256,768]{2,1,0:T(8,128)(2,1)S(1)} %get-tuple-element.35.x, bf16[768,768]{1,0:T(8,128)(2,1)S(1)} %copy-done, bf16[768,768]{1,0:T(8,128)(2,1)S(1)} %copy-done.1), custom_call_target="tpu_custom_call" | custom-call | flops 2415919104 | bytes 6000000 | tf_op jit(solution)/shard_map/pallas_call | solution.py:371
  51.8 0.1 collective-permute-start.9
  51.9 0.4 collective-permute-start.12
  52.4 0.1 collective-permute-start.11
  52.5 0.4 collective-permute-start.10
  52.9 1.6 %shard_map.85.grads = bf16[1024,1024]{1,0:T(8,128)(2,1)S(1)} custom-call(s32[2]{0:T(128)S(1)} %pad_add_fusion.sc, bf16[2,8,16,256]{3,2,1,0:T(8,128)(2,1)S(1)} %maximum_bitcast_fusion.refs_0_, bf16[2,8,16,256]{3,2,1,0:T(8,128)(2,1)S(1)} %collective-permute-done.19.refs_1_, bf16[2,8,16,256]{3,2,1,0:T(8,128)(2,1)S(1)} %collective-permute-done.20.refs_2_, ...), custom_call_target="tpu_custom_call" | custom-call | flops 536870912 | bytes 4000000 | tf_op jit(solution)/shard_map/pallas_call | solution.py:432
  54.5 1.8 %shard_map.86.refs_12_ = f32[4,256,768]{2,1,0:T(8,128)S(1)} custom-call(bf16[1024,1024]{1,0:T(8,128)(2,1)S(1)} %shard_map.85.grads, bf16[768,768]{1,0:T(8,128)(2,1)S(1)} %copy-done, bf16[768,768]{1,0:T(8,128)(2,1)S(1)} %copy-done.1, f32[4,256,768]{2,1,0:T(8,128)S(1)} %get-tuple-element.60.o_in), custom_call_target="tpu_custom_call" | custom-call | flops 1610612736 | bytes 6000000 | tf_op jit(solution)/shard_map/pallas_call | solution.py:440
  56.4 3.2 %shard_map.87 = f32[4,256,768]{2,1,0:T(8,128)} custom-call(s32[2]{0:T(128)S(1)} %pad_add_fusion.sc, bf16[2,4,16,256]{3,2,1,0:T(8,128)(2,1)S(1)} %maximum_bitcast_fusion.1.refs_0_, bf16[2,4,16,256]{3,2,1,0:T(8,128)(2,1)S(1)} %collective-permute-done.6.refs_1_, bf16[2,4,16,256]{3,2,1,0:T(8,128)(2,1)S(1)} %collective-permute-done.7.refs_2_, ...), custom_call_target="tpu_custom_call" | custom-call | flops 1073741824 | bytes 4000000 | tf_op jit(solution)/shard_map/pallas_call | solution.py:417
  (28 shorter events, 0.1 us)
Async XLA Ops:
  4.9 3.9 %collective-permute-start.13 = (bf16[8,8,16,256]{3,2,1,0:T(8,128)(2,1)S(1)}, bf16[8,8,16,256]{3,2,1,0:T(8,128)(2,1)S(1)}, u32[]{:S(2)}, u32[]{:S(2)}) collective-permute-start(bf16[8,8,16,256]{3,2,1,0:T(8,128)(2,1)S(1)} %get-tuple-element.53), channel_id=1, source_target_pairs={{0,1},{1,0},{2,3},{3,2},{4,5},{5,4},{6,7},{7,6},{8,9},{9,8},{10,11... | collective-permute-start | bytes 1572872 | tf_op jit(solution)/shard_map/ppermute | solution.py:273
  8.6 5.7 %collective-permute-start = (bf16[8,4,16,256]{3,2,1,0:T(8,128)(2,1)S(1)}, bf16[8,4,16,256]{3,2,1,0:T(8,128)(2,1)S(1)}, u32[]{:S(2)}, u32[]{:S(2)}) collective-permute-start(bf16[8,4,16,256]{3,2,1,0:T(8,128)(2,1)S(1)} %get-tuple-element.42), channel_id=1, source_target_pairs={{0,1},{1,0},{2,3},{3,2},{4,5},{5,4},{6,7},{7,6},{8,9},{9,8},{10,11... | collective-permute-start | bytes 786440 | tf_op jit(solution)/shard_map/ppermute | solution.py:273
  8.7 14.8 %copy-start.2 = (f32[256,12,256]{2,0,1:T(8,128)S(1)}, f32[256,12,256]{2,0,1:T(8,128)}, u32[]{:S(2)}) copy-start(f32[256,12,256]{2,0,1:T(8,128)} %param.13) | copy-start | bytes 9437188
  8.9 9.1 %collective-permute-start.14 = (bf16[2,8,16,256]{3,2,1,0:T(8,128)(2,1)S(1)}, bf16[2,8,16,256]{3,2,1,0:T(8,128)(2,1)S(1)}, u32[]{:S(2)}, u32[]{:S(2)}) collective-permute-start(bf16[2,8,16,256]{3,2,1,0:T(8,128)(2,1)S(1)} %get-tuple-element.55), channel_id=1, source_target_pairs={{0,2},{2,0},{4,6},{6,4},{8,10},{10,8},{12,14},{14,12},{1,3},{3,1},... | collective-permute-start | bytes 393224 | tf_op jit(solution)/shard_map/ppermute | solution.py:273
  11.9 6.5 %collective-permute-start.15 = (bf16[2,8,16,256]{3,2,1,0:T(8,128)(2,1)S(1)}, bf16[2,8,16,256]{3,2,1,0:T(8,128)(2,1)S(1)}, u32[]{:S(2)}, u32[]{:S(2)}) collective-permute-start(bf16[2,8,16,256]{3,2,1,0:T(8,128)(2,1)S(1)} %get-tuple-element.56), channel_id=1, source_target_pairs={{0,4},{2,6},{4,0},{6,2},{8,12},{10,14},{12,8},{14,10},{1,5},{3,7},... | collective-permute-start | bytes 393224 | tf_op jit(solution)/shard_map/ppermute | solution.py:273
  13.5 7.3 %collective-permute-start.16 = (bf16[2,8,16,256]{3,2,1,0:T(8,128)(2,1)S(1)}, bf16[2,8,16,256]{3,2,1,0:T(8,128)(2,1)S(1)}, u32[]{:S(2)}, u32[]{:S(2)}) collective-permute-start(bf16[2,8,16,256]{3,2,1,0:T(8,128)(2,1)S(1)} %get-tuple-element.57), channel_id=1, source_target_pairs={{0,6},{2,4},{4,2},{6,0},{8,14},{10,12},{12,10},{14,8},{1,7},{3,5},... | collective-permute-start | bytes 393224 | tf_op jit(solution)/shard_map/ppermute | solution.py:273
  14.4 14.5 %collective-permute-start.1 = (bf16[2,4,16,256]{3,2,1,0:T(8,128)(2,1)S(1)}, bf16[2,4,16,256]{3,2,1,0:T(8,128)(2,1)S(1)}, u32[]{:S(2)}, u32[]{:S(2)}) collective-permute-start(bf16[2,4,16,256]{3,2,1,0:T(8,128)(2,1)S(1)} %get-tuple-element.44), channel_id=1, source_target_pairs={{0,2},{2,0},{4,6},{6,4},{8,10},{10,8},{12,14},{14,12},{1,3},{3,1},... | collective-permute-start | bytes 196616 | tf_op jit(solution)/shard_map/ppermute | solution.py:273
  16.4 12.5 %collective-permute-start.2 = (bf16[2,4,16,256]{3,2,1,0:T(8,128)(2,1)S(1)}, bf16[2,4,16,256]{3,2,1,0:T(8,128)(2,1)S(1)}, u32[]{:S(2)}, u32[]{:S(2)}) collective-permute-start(bf16[2,4,16,256]{3,2,1,0:T(8,128)(2,1)S(1)} %get-tuple-element.45), channel_id=1, source_target_pairs={{0,4},{2,6},{4,0},{6,2},{8,12},{10,14},{12,8},{14,10},{1,5},{3,7},... | collective-permute-start | bytes 196616 | tf_op jit(solution)/shard_map/ppermute | solution.py:273
  18.0 10.9 %collective-permute-start.3 = (bf16[2,4,16,256]{3,2,1,0:T(8,128)(2,1)S(1)}, bf16[2,4,16,256]{3,2,1,0:T(8,128)(2,1)S(1)}, u32[]{:S(2)}, u32[]{:S(2)}) collective-permute-start(bf16[2,4,16,256]{3,2,1,0:T(8,128)(2,1)S(1)} %get-tuple-element.46), channel_id=1, source_target_pairs={{0,6},{2,4},{4,2},{6,0},{8,14},{10,12},{12,10},{14,8},{1,7},{3,5},... | collective-permute-start | bytes 196616 | tf_op jit(solution)/shard_map/ppermute | solution.py:273
  20.8 5.2 %collective-permute-start.17 = (bf16[8,16,256]{2,1,0:T(8,128)(2,1)S(1)}, bf16[8,16,256]{2,1,0:T(8,128)(2,1)S(1)}, u32[]{:S(2)}, u32[]{:S(2)}) collective-permute-start(bf16[8,16,256]{2,1,0:T(8,128)(2,1)S(1)} %get-tuple-element.59), channel_id=1, source_target_pairs={{0,8},{2,10},{4,12},{6,14},{8,0},{10,2},{12,4},{14,6},{1,9},{3,11}... | collective-permute-start | bytes 196616 | tf_op jit(solution)/shard_map/ppermute | solution.py:273
  23.5 25.6 %copy-start = (bf16[768,768]{1,0:T(8,128)(2,1)S(1)}, bf16[768,768]{1,0:T(8,128)(2,1)}, u32[]{:S(2)}) copy-start(bf16[768,768]{1,0:T(8,128)(2,1)} %refs_10_.1) | copy-start | bytes 3538948
  23.5 25.6 %copy-start.1 = (bf16[768,768]{1,0:T(8,128)(2,1)S(1)}, bf16[768,768]{1,0:T(8,128)(2,1)}, u32[]{:S(2)}) copy-start(bf16[768,768]{1,0:T(8,128)(2,1)} %refs_11_.1) | copy-start | bytes 3538948
  26.1 8.5 %collective-permute-start.18 = (bf16[1,8,16,256]{3,2,1,0:T(8,128)(2,1)S(1)}, bf16[1,8,16,256]{3,2,1,0:T(8,128)(2,1)S(1)}, u32[]{:S(2)}, u32[]{:S(2)}) collective-permute-start(bf16[1,8,16,256]{3,2,1,0:T(8,128)(2,1)S(1)} %bitcast.21), channel_id=1, source_target_pairs={{0,8},{2,10},{4,12},{6,14},{8,0},{10,2},{12,4},{14,6},{1,9},{3,11}... | collective-permute-start | bytes 196616 | tf_op jit(solution)/shard_map/ppermute | solution.py:273
  28.9 5.2 %collective-permute-start.4 = (bf16[4,16,256]{2,1,0:T(8,128)(2,1)S(1)}, bf16[4,16,256]{2,1,0:T(8,128)(2,1)S(1)}, u32[]{:S(2)}, u32[]{:S(2)}) collective-permute-start(bf16[4,16,256]{2,1,0:T(8,128)(2,1)S(1)} %get-tuple-element.48), channel_id=1, source_target_pairs={{0,8},{2,10},{4,12},{6,14},{8,0},{10,2},{12,4},{14,6},{1,9},{3,11}... | collective-permute-start | bytes 98312 | tf_op jit(solution)/shard_map/ppermute | solution.py:273
  34.2 5.8 %collective-permute-start.5 = (bf16[1,4,16,256]{3,2,1,0:T(8,128)(2,1)S(1)}, bf16[1,4,16,256]{3,2,1,0:T(8,128)(2,1)S(1)}, u32[]{:S(2)}, u32[]{:S(2)}) collective-permute-start(bf16[1,4,16,256]{3,2,1,0:T(8,128)(2,1)S(1)} %bitcast.23), channel_id=1, source_target_pairs={{0,8},{2,10},{4,12},{6,14},{8,0},{10,2},{12,4},{14,6},{1,9},{3,11}... | collective-permute-start | bytes 98312 | tf_op jit(solution)/shard_map/ppermute | solution.py:273
  34.7 13.4 %collective-permute-start.21 = (bf16[2,8,16,256]{3,2,1,0:T(8,128)(2,1)S(1)}, bf16[2,8,16,256]{3,2,1,0:T(8,128)(2,1)S(1)}, u32[]{:S(2)}, u32[]{:S(2)}) collective-permute-start(bf16[2,8,16,256]{3,2,1,0:T(8,128)(2,1)S(1)} %maximum_bitcast_fusion.refs_0_), channel_id=1, source_target_pairs={{0,6},{2,4},{4,2},{6,0},{8,14},{10,12},{12,10},{14,8},{1,7},{3,5},... | collective-permute-start | bytes 393224 | tf_op jit(solution)/shard_map/ppermute | solution.py:273
  39.4 9.2 %collective-permute-start.20 = (bf16[2,8,16,256]{3,2,1,0:T(8,128)(2,1)S(1)}, bf16[2,8,16,256]{3,2,1,0:T(8,128)(2,1)S(1)}, u32[]{:S(2)}, u32[]{:S(2)}) collective-permute-start(bf16[2,8,16,256]{3,2,1,0:T(8,128)(2,1)S(1)} %maximum_bitcast_fusion.refs_0_), channel_id=1, source_target_pairs={{0,4},{2,6},{4,0},{6,2},{8,12},{10,14},{12,8},{14,10},{1,5},{3,7},... | collective-permute-start | bytes 393224 | tf_op jit(solution)/shard_map/ppermute | solution.py:273
  39.4 9.3 %collective-permute-start.19 = (bf16[2,8,16,256]{3,2,1,0:T(8,128)(2,1)S(1)}, bf16[2,8,16,256]{3,2,1,0:T(8,128)(2,1)S(1)}, u32[]{:S(2)}, u32[]{:S(2)}) collective-permute-start(bf16[2,8,16,256]{3,2,1,0:T(8,128)(2,1)S(1)} %maximum_bitcast_fusion.refs_0_), channel_id=1, source_target_pairs={{0,2},{2,0},{4,6},{6,4},{8,10},{10,8},{12,14},{14,12},{1,3},{3,1},... | collective-permute-start | bytes 393224 | tf_op jit(solution)/shard_map/ppermute | solution.py:273
  40.0 6.0 %collective-permute-start.8 = (bf16[2,4,16,256]{3,2,1,0:T(8,128)(2,1)S(1)}, bf16[2,4,16,256]{3,2,1,0:T(8,128)(2,1)S(1)}, u32[]{:S(2)}, u32[]{:S(2)}) collective-permute-start(bf16[2,4,16,256]{3,2,1,0:T(8,128)(2,1)S(1)} %maximum_bitcast_fusion.1.refs_0_), channel_id=1, source_target_pairs={{0,6},{2,4},{4,2},{6,0},{8,14},{10,12},{12,10},{14,8},{1,7},{3,5},... | collective-permute-start | bytes 196616 | tf_op jit(solution)/shard_map/ppermute | solution.py:273
  43.8 4.3 %collective-permute-start.7 = (bf16[2,4,16,256]{3,2,1,0:T(8,128)(2,1)S(1)}, bf16[2,4,16,256]{3,2,1,0:T(8,128)(2,1)S(1)}, u32[]{:S(2)}, u32[]{:S(2)}) collective-permute-start(bf16[2,4,16,256]{3,2,1,0:T(8,128)(2,1)S(1)} %maximum_bitcast_fusion.1.refs_0_), channel_id=1, source_target_pairs={{0,4},{2,6},{4,0},{6,2},{8,12},{10,14},{12,8},{14,10},{1,5},{3,7},... | collective-permute-start | bytes 196616 | tf_op jit(solution)/shard_map/ppermute | solution.py:273
  46.0 5.8 %collective-permute-start.6 = (bf16[2,4,16,256]{3,2,1,0:T(8,128)(2,1)S(1)}, bf16[2,4,16,256]{3,2,1,0:T(8,128)(2,1)S(1)}, u32[]{:S(2)}, u32[]{:S(2)}) collective-permute-start(bf16[2,4,16,256]{3,2,1,0:T(8,128)(2,1)S(1)} %maximum_bitcast_fusion.1.refs_0_), channel_id=1, source_target_pairs={{0,2},{2,0},{4,6},{6,4},{8,10},{10,8},{12,14},{14,12},{1,3},{3,1},... | collective-permute-start | bytes 196616 | tf_op jit(solution)/shard_map/ppermute | solution.py:273
  48.1 3.9 %collective-permute-start.22 = (bf16[2,8,16,256]{3,2,1,0:T(8,128)(2,1)S(1)}, bf16[2,8,16,256]{3,2,1,0:T(8,128)(2,1)S(1)}, u32[]{:S(2)}, u32[]{:S(2)}) collective-permute-start(bf16[2,8,16,256]{3,2,1,0:T(8,128)(2,1)S(1)} %maximum_bitcast_fusion.refs_0_), channel_id=1, source_target_pairs={{0,1},{1,0},{2,3},{3,2},{4,5},{5,4},{6,7},{7,6},{8,9},{9,8},{10,11... | collective-permute-start | bytes 393224 | tf_op jit(solution)/shard_map/ppermute | solution.py:273
  48.1 4.3 %collective-permute-start.25 = (bf16[2,8,16,256]{3,2,1,0:T(8,128)(2,1)S(1)}, bf16[2,8,16,256]{3,2,1,0:T(8,128)(2,1)S(1)}, u32[]{:S(2)}, u32[]{:S(2)}) collective-permute-start(bf16[2,8,16,256]{3,2,1,0:T(8,128)(2,1)S(1)} %collective-permute-done.21.refs_3_), channel_id=1, source_target_pairs={{0,1},{1,0},{2,3},{3,2},{4,5},{5,4},{6,7},{7,6},{8,9},{9,8},{10,11... | collective-permute-start | bytes 393224 | tf_op jit(solution)/shard_map/ppermute | solution.py:273
  48.6 3.9 %collective-permute-start.24 = (bf16[2,8,16,256]{3,2,1,0:T(8,128)(2,1)S(1)}, bf16[2,8,16,256]{3,2,1,0:T(8,128)(2,1)S(1)}, u32[]{:S(2)}, u32[]{:S(2)}) collective-permute-start(bf16[2,8,16,256]{3,2,1,0:T(8,128)(2,1)S(1)} %collective-permute-done.20.refs_2_), channel_id=1, source_target_pairs={{0,1},{1,0},{2,3},{3,2},{4,5},{5,4},{6,7},{7,6},{8,9},{9,8},{10,11... | collective-permute-start | bytes 393224 | tf_op jit(solution)/shard_map/ppermute | solution.py:273
  48.6 4.3 %collective-permute-start.23 = (bf16[2,8,16,256]{3,2,1,0:T(8,128)(2,1)S(1)}, bf16[2,8,16,256]{3,2,1,0:T(8,128)(2,1)S(1)}, u32[]{:S(2)}, u32[]{:S(2)}) collective-permute-start(bf16[2,8,16,256]{3,2,1,0:T(8,128)(2,1)S(1)} %collective-permute-done.19.refs_1_), channel_id=1, source_target_pairs={{0,1},{1,0},{2,3},{3,2},{4,5},{5,4},{6,7},{7,6},{8,9},{9,8},{10,11... | collective-permute-start | bytes 393224 | tf_op jit(solution)/shard_map/ppermute | solution.py:273
  51.8 4.6 %collective-permute-start.9 = (bf16[2,4,16,256]{3,2,1,0:T(8,128)(2,1)S(1)}, bf16[2,4,16,256]{3,2,1,0:T(8,128)(2,1)S(1)}, u32[]{:S(2)}, u32[]{:S(2)}) collective-permute-start(bf16[2,4,16,256]{3,2,1,0:T(8,128)(2,1)S(1)} %maximum_bitcast_fusion.1.refs_0_), channel_id=1, source_target_pairs={{0,1},{1,0},{2,3},{3,2},{4,5},{5,4},{6,7},{7,6},{8,9},{9,8},{10,11... | collective-permute-start | bytes 196616 | tf_op jit(solution)/shard_map/ppermute | solution.py:273
  51.9 4.5 %collective-permute-start.12 = (bf16[2,4,16,256]{3,2,1,0:T(8,128)(2,1)S(1)}, bf16[2,4,16,256]{3,2,1,0:T(8,128)(2,1)S(1)}, u32[]{:S(2)}, u32[]{:S(2)}) collective-permute-start(bf16[2,4,16,256]{3,2,1,0:T(8,128)(2,1)S(1)} %collective-permute-done.8.refs_3_), channel_id=1, source_target_pairs={{0,1},{1,0},{2,3},{3,2},{4,5},{5,4},{6,7},{7,6},{8,9},{9,8},{10,11... | collective-permute-start | bytes 196616 | tf_op jit(solution)/shard_map/ppermute | solution.py:273
  52.4 4.0 %collective-permute-start.11 = (bf16[2,4,16,256]{3,2,1,0:T(8,128)(2,1)S(1)}, bf16[2,4,16,256]{3,2,1,0:T(8,128)(2,1)S(1)}, u32[]{:S(2)}, u32[]{:S(2)}) collective-permute-start(bf16[2,4,16,256]{3,2,1,0:T(8,128)(2,1)S(1)} %collective-permute-done.7.refs_2_), channel_id=1, source_target_pairs={{0,1},{1,0},{2,3},{3,2},{4,5},{5,4},{6,7},{7,6},{8,9},{9,8},{10,11... | collective-permute-start | bytes 196616 | tf_op jit(solution)/shard_map/ppermute | solution.py:273
  52.5 3.9 %collective-permute-start.10 = (bf16[2,4,16,256]{3,2,1,0:T(8,128)(2,1)S(1)}, bf16[2,4,16,256]{3,2,1,0:T(8,128)(2,1)S(1)}, u32[]{:S(2)}, u32[]{:S(2)}) collective-permute-start(bf16[2,4,16,256]{3,2,1,0:T(8,128)(2,1)S(1)} %collective-permute-done.6.refs_1_), channel_id=1, source_target_pairs={{0,1},{1,0},{2,3},{3,2},{4,5},{5,4},{6,7},{7,6},{8,9},{9,8},{10,11... | collective-permute-start | bytes 196616 | tf_op jit(solution)/shard_map/ppermute | solution.py:273
